TPU v7x, 512 devices: a whole 4x4x16 slice. The times are simulated.
512 devices in a mesh: gx: 64 (over x, y, z_hi), gy: 8 (over z_lo, core).
Axes of the slice: x: 4, y: 4, z: 16 (z_hi: 4, z_lo: 4; z = z_hi * 4 + z_lo), core: 2. Of those that a mesh axis runs over, the one named last changes fastest.
Arguments:
- positions: float32 [3, 512, 32, 4], P(None, 'gx', 'gy'), may hold values from 0 to 1536, as said below
- occupied: int32 [512, 32, 4], P('gx', 'gy'), may hold values from 0 to 1
- species: int32 [512, 32, 4], P('gx', 'gy'), may hold values from 0 to 9
- neighbours: int32 [512, 32, 4, 12], P('gx', 'gy'), may hold values from 0 to 383, as said below
- embedding: bfloat16 [10, 128], replicated, may hold values from -6 to 6
- radial_first: bfloat16 [2, 8, 64], replicated, may hold values from -6 to 6
- radial_second: bfloat16 [2, 64, 64], replicated, may hold values from -0.75 to 0.75
- radial_third: bfloat16 [2, 64, 64], replicated, may hold values from -0.75 to 0.75
- radial_last: bfloat16 [2, 64, 384], replicated, may hold values from -1.5 to 1.5
- up_weight: bfloat16 [2, 128, 128], replicated, may hold values from -0.5 to 0.5
- product_weight: float32 [2, 10, 4, 128], replicated, may hold values from -3 to 3
- out_weight: bfloat16 [2, 128, 128], replicated, may hold values from -0.5 to 0.5
- read_linear: float32 [1, 128], replicated, may hold values from -0.5 to 0.5
- read_hidden: bfloat16 [128, 16], replicated, may hold values from -0.5 to 0.5
- read_last: float32 [16], replicated, may hold values from -1.5 to 1.5
Outputs:
- energies: float32 [512, 32, 4], P('gx', 'gy')
- forces: float32 [3, 512, 32, 4], P(None, 'gx', 'gy')
Inputs may be any that keep to these rules, and one draw needn't show every extreme that they name: `positions`: each coordinate of site (x, y, z) lies within 0.22 * 2.2 of its site's centre 2.2 (x + 0.5, y + 0.5, z + 0.5). `neighbours`: a site's 12 slots name distinct other sites inside the depth range whose offset (dx, dy, dz) in sites has dx^2 + dy^2 + dz^2 <= 5, as (p * 8 + q) * 4 + s in the block of its domain extended by two sites on each side along the long axis and across.
All inputs are finite; a program needn't handle non-finite values.
Results may differ from a plain program's by a relative error of at most 0.035.
Values may be sent and summed in bfloat16 or wider, within the bound.
A program may use at most 64 MiB of HBM per device.

v0:
```python
import math

import jax
import jax.numpy as jnp
from jax import lax
from jax.experimental import pallas as pl
from jax.experimental.pallas import tpu as pltpu
from jax.sharding import PartitionSpec as P

F32 = jnp.float32
BF16 = jnp.bfloat16
MESH = pl.DeviceIdType.MESH
CUTOFF = 5.0
SLOTS = 12
SITES = 128
EDGES = SITES * SLOTS
GHOSTS = 256
EXT = SITES + GHOSTS
CH = 128
RAD = 64
BES = 8
LAYERS = 2

DIRS = ((-1, 0), (1, 0), (-1, -1), (-1, 1), (1, -1), (1, 1), (0, -1), (0, 1))
OFF = (0, 32, 64, 80, 96, 112, 128, 192)
LEN = (32, 32, 16, 16, 16, 16, 64, 64)
OPP = (1, 0, 5, 4, 3, 2, 7, 6)

NT = (((1,), (1,)), ((), ()))
TN = (((0,), (0,)), ((), ()))
NN = (((1,), (0,)), ((), ()))


def dot(a, b, dims=NN):
    return lax.dot_general(a, b, dims, preferred_element_type=F32)


def dot_exact(a, b, dims=NN):
    return lax.dot_general(a, b, dims, preferred_element_type=F32, precision=lax.Precision.HIGHEST)


def iota(shape, dim):
    return lax.broadcasted_iota(jnp.int32, shape, dim)


def split3(x):
    high = x.astype(BF16).astype(F32)
    rest = x - high
    middle = rest.astype(BF16).astype(F32)
    return jnp.concatenate([high, middle, rest - middle], axis=0).astype(BF16)


def split2(x):
    high = x.astype(BF16).astype(F32)
    return jnp.concatenate([high, x - high], axis=0).astype(BF16)


def strip_site(direction, row):
    dx, dy = DIRS[direction]
    per_x = 16 if dy == 0 else 8
    x0 = 6 if dx == 1 else 0
    y0 = 2 if dy == 1 else 0
    return (x0 + row // per_x) * 16 + y0 * 4 + row % per_x


def silu_parts(z):
    s = 0.5 + 0.5 * jnp.tanh(0.5 * z)
    g = z * s
    return g, s + g * (1.0 - s)


ROOT3 = math.sqrt(3.0)
ROOT5 = math.sqrt(5.0)
ROOT15 = math.sqrt(15.0)
FACTOR = 1.0 / math.sqrt(SLOTS)


def kernel(
    n_gx,
    n_gy,
    pos_ref,
    occ_ref,
    spec_ref,
    nbr_ref,
    emb_ref,
    w1_ref,
    w2_ref,
    w3_ref,
    w4_ref,
    up_ref,
    pw_ref,
    ow_ref,
    rl_ref,
    rh_ref,
    rlast_ref,
    en_ref,
    force_ref,
    raw,
    nb,
    geo,
    sel,
    ps,
    oh,
    snd1,
    rcv1,
    snd2,
    rcv2,
    snd3,
    rcv3,
    snd4,
    rcv4,
    gs,
    bs,
    ye,
    bd,
    mix,
    dsilu,
    q,
    u,
    a,
    msg,
    dq,
    du,
    s_acc,
    send_sem,
    recv_sem,
):
    gx = lax.axis_index("gx")
    gy = lax.axis_index("gy")
    peers = []
    inside = []
    for dx, dy in DIRS:
        px, py = gx + dx, gy + dy
        peers.append((lax.rem(px + n_gx, n_gx), lax.rem(py + n_gy, n_gy)))
        inside.append((px >= 0) & (px < n_gx) & (py >= 0) & (py < n_gy))

    barrier = pltpu.get_barrier_semaphore()
    for peer in peers:
        pl.semaphore_signal(barrier, inc=1, device_id=peer, device_id_type=MESH)

    raw[...] = jnp.zeros_like(raw)
    for y in range(4):
        for c in range(3):
            raw[c * 16 + y * 4 : c * 16 + y * 4 + 4, 0:8] = pos_ref[c, y]
        raw[48 + y * 4 : 52 + y * 4, 0:8] = occ_ref[y].astype(F32)
        raw[64 + y * 4 : 68 + y * 4, 0:8] = spec_ref[y].astype(F32)
    x_pick = (iota((SITES, SITES), 0) == iota((SITES, SITES), 1) // 16).astype(F32)
    spread = dot_exact(raw[...], x_pick)
    yz_mask = iota((80, SITES), 0) % 16 == iota((80, SITES), 1) % 16
    spread = jnp.where(yz_mask, spread, 0.0)
    geo[...] = jnp.zeros_like(geo)
    for f in range(5):
        geo[f : f + 1, 0:SITES] = jnp.sum(spread[f * 16 : f * 16 + 16], axis=0, keepdims=True)

    lane = iota((SITES, SITES), 1)
    site = iota((SITES, SITES), 0)
    for d in range(8):
        row = lane - OFF[OPP[d]] % SITES
        hit = (row >= 0) & (row < LEN[d]) & (strip_site(d, row) == site)
        sel[:, d * SITES : (d + 1) * SITES] = jnp.where(hit, 1.0, 0.0).astype(BF16)
        rows = iota((LEN[d], SITES), 0)
        hit = strip_site(d, rows) == iota((LEN[d], SITES), 1)
        ps[OFF[d] : OFF[d] + LEN[d], :] = jnp.where(hit, 1.0, 0.0).astype(BF16)
    placed = dot(split3(geo[:, 0:SITES]), sel[...])
    placed = placed[0:8] + placed[8:16] + placed[16:24]
    for d in range(8):
        snd1[d] = placed[:, d * SITES : (d + 1) * SITES]

    pl.semaphore_wait(barrier, 8)

    copies = []

    def exchange(phase, sources, targets):
        started = []
        for d in range(8):
            copy = pltpu.make_async_remote_copy(
                src_ref=sources(d),
                dst_ref=targets(OPP[d]),
                send_sem=send_sem.at[phase, d],
                recv_sem=recv_sem.at[phase, OPP[d]],
                device_id=peers[d],
                device_id_type=MESH,
            )
            copy.start()
            started.append(copy)
        copies.extend(started)

        def finish():
            for d in range(8):
                pltpu.make_async_remote_copy(
                    src_ref=sources(OPP[d]),
                    dst_ref=targets(d),
                    send_sem=send_sem.at[phase, OPP[d]],
                    recv_sem=recv_sem.at[phase, d],
                    device_id=peers[OPP[d]],
                    device_id_type=MESH,
                ).wait_recv()

        return finish

    arrived1 = exchange(0, lambda d: snd1.at[d], lambda d: rcv1.at[d])

    nb[...] = jnp.zeros_like(nb)
    for x in range(8):
        for y in range(4):
            nb[x * 16 + y * 4 : x * 16 + y * 4 + 4, 0:SLOTS] = nbr_ref[x, y].astype(F32)
    index = nb[...].T[0:16].astype(jnp.int32)
    s = index & 3
    yy = (index >> 2) & 7
    xx = index >> 5
    x_lo, x_hi, y_lo, y_hi = xx < 2, xx >= 10, yy < 2, yy >= 6
    rx = jnp.where(x_lo, xx, jnp.where(x_hi, xx - 10, xx - 2))
    ry = jnp.where(y_lo, yy, jnp.where(y_hi, yy - 6, yy - 2))
    per_x = jnp.where(y_lo | y_hi, 8, 16)
    base_lo = jnp.where(y_lo, OFF[2], jnp.where(y_hi, OFF[3], OFF[0]))
    base_hi = jnp.where(y_lo, OFF[4], jnp.where(y_hi, OFF[5], OFF[1]))
    base_mid = jnp.where(y_lo, OFF[6], jnp.where(y_hi, OFF[7], -SITES))
    base = jnp.where(x_lo, base_lo, jnp.where(x_hi, base_hi, base_mid))
    place = base + SITES + rx * per_x + ry * 4 + s
    ext_row = iota((EXT, SITES), 0)
    for k in range(SLOTS):
        hit = ext_row == place[k : k + 1]
        oh[:, k * SITES : (k + 1) * SITES] = jnp.where(hit, 1.0, 0.0).astype(BF16)

    present = geo[3:4, 0:SITES]
    own_hot = (geo[4:5, 0:SITES].astype(jnp.int32) == iota((16, SITES), 0)).astype(F32)
    for layer in range(LAYERS):
        for j in range(4):
            table = pw_ref[layer, :, j, :]
            mix[layer, j] = dot_exact(table, own_hot[0:10], TN)
    h0 = dot(emb_ref[...].astype(F32), own_hot[0:10], TN) * present
    lifted_table = dot(emb_ref[...], up_ref[0]).astype(BF16).astype(F32)

    arrived1()
    for f in range(2):
        tile = jnp.zeros((8, SITES), F32)
        for d in range(8):
            if OFF[d] // SITES == f:
                tile = tile + jnp.where(inside[d], rcv1[d], 0.0)
        geo[:, (f + 1) * SITES : (f + 2) * SITES] = tile

    gathered = dot(split3(geo[...]), oh[...])
    gathered = gathered[0:8] + gathered[8:16] + gathered[16:24]
    for k in range(SLOTS):
        gs[k * 8 : k * 8 + 8, :] = gathered[:, k * SITES : (k + 1) * SITES]
    ext_hot = (geo[4:5, :].astype(jnp.int32) == iota((16, EXT), 0)).astype(F32)
    u0 = dot(lifted_table, ext_hot[0:10], TN).astype(BF16)
    u[0] = dot(u0, oh[...])

    def rows_of(ref, m):
        return ref[pl.ds(m, SLOTS, stride=8), :]

    disp = [rows_of(gs, c) - geo[c : c + 1, 0:SITES] for c in range(3)]
    w = rows_of(gs, 3) * present
    squared = disp[0] * disp[0] + disp[1] * disp[1] + disp[2] * disp[2]
    dist = jnp.sqrt(jnp.where(w > 0, squared, 1.0))
    inv = 1.0 / dist
    nx, ny, nz = [c * inv for c in disp]
    scaled = jnp.minimum(dist * (1.0 / CUTOFF), 1.0)
    u2 = scaled * scaled
    u5 = u2 * u2 * scaled
    u6 = u5 * scaled
    env = 1.0 - 28.0 * u6 + 48.0 * u6 * scaled - 21.0 * u6 * u2
    env = jnp.where(scaled < 1.0, env, 0.0)
    gap = 1.0 - scaled
    slope = (-168.0 / CUTOFF) * u5 * gap * gap
    env_w = env * w
    slope_w = slope * w
    ye_scale = FACTOR * env_w
    harmonics = [
        ROOT3 * nx,
        ROOT3 * ny,
        ROOT3 * nz,
        ROOT15 * nx * ny,
        ROOT15 * ny * nz,
        0.5 * ROOT5 * (3.0 * nz * nz - 1.0),
        ROOT15 * nx * nz,
        0.5 * ROOT15 * (nx * nx - ny * ny),
    ]
    ye[0, 0:SLOTS] = ye_scale
    for m in range(8):
        ye[m + 1, 0:SLOTS] = ye_scale * harmonics[m]
    theta = math.pi * scaled
    sin1 = jnp.sin(theta)
    cos1 = jnp.cos(theta)
    twice = 2.0 * cos1
    sin_before, cos_before = jnp.zeros_like(sin1), jnp.ones_like(cos1)
    sin_m, cos_m = sin1, cos1
    amplitude = math.sqrt(2.0 / CUTOFF) * inv
    for m in range(BES):
        value = amplitude * sin_m
        bs[pl.ds(m, SLOTS, stride=8), :] = value
        bd[m, 0:SLOTS] = amplitude * ((m + 1) * math.pi / CUTOFF) * cos_m - value * inv
        sin_m, sin_before = twice * sin_m - sin_before, sin_m
        cos_m, cos_before = twice * cos_m - cos_before, cos_m

    def radial(layer):
        hidden = jnp.concatenate([bs[k * 8 : k * 8 + 8, :] for k in range(SLOTS)], axis=1)
        hidden = hidden.astype(BF16)
        for step, ref in enumerate((w1_ref, w2_ref, w3_ref)):
            z = dot(ref[layer], hidden, TN)
            g, slope_g = silu_parts(z)
            dsilu[layer, step] = slope_g
            hidden = g.astype(BF16)
        q[layer] = dot(w4_ref[layer], hidden, TN)

    def aggregate(layer):
        def body(block, carry):
            c0 = pl.multiple_of(block * 32, 32)
            acc = [jnp.zeros((32, SITES), F32) for _ in range(9)]
            for k in range(SLOTS):
                lanes = slice(k * SITES, (k + 1) * SITES)
                uk = u[layer, pl.ds(c0, 32), lanes]
                v = [q[layer, pl.ds(L * CH + c0, 32), lanes] * uk for L in range(3)]
                for m in range(9):
                    degree = 0 if m == 0 else (1 if m < 4 else 2)
                    acc[m] = acc[m] + ye[m, k : k + 1, :] * v[degree]
            for m in range(9):
                a[layer, m, pl.ds(c0, 32), :] = acc[m]
            p = [mix[layer, j, pl.ds(c0, 32), :] for j in range(4)]
            first = acc[1] * acc[1] + acc[2] * acc[2] + acc[3] * acc[3]
            second = acc[4] * acc[4] + acc[5] * acc[5] + acc[6] * acc[6]
            second = second + acc[7] * acc[7] + acc[8] * acc[8]
            result = p[0] * acc[0] + p[1] * acc[0] * acc[0] + p[2] * first + p[3] * second
            msg[pl.ds(c0, 32), :] = result.astype(BF16)
            return carry

        lax.fori_loop(0, CH // 32, body, 0)

    def aggregate_back(layer, msg_grad_ref, with_du):
        def body(block, carry):
            c0 = pl.multiple_of(block * 32, 32)
            g = msg_grad_ref[pl.ds(c0, 32), :]
            p = [mix[layer, j, pl.ds(c0, 32), :] for j in range(4)]
            a0 = a[layer, 0, pl.ds(c0, 32), :]
            scale1 = 2.0 * p[2] * g
            scale2 = 2.0 * p[3] * g
            da = [g * (p[0] + 2.0 * p[1] * a0)]
            for m in range(1, 9):
                da.append((scale1 if m < 4 else scale2) * a[layer, m, pl.ds(c0, 32), :])
            for k in range(SLOTS):
                lanes = slice(k * SITES, (k + 1) * SITES)
                uk = u[layer, pl.ds(c0, 32), lanes]
                qk = [q[layer, pl.ds(L * CH + c0, 32), lanes] for L in range(3)]
                v = [one * uk for one in qk]
                dv = [None, None, None]
                for m in range(9):
                    degree = 0 if m == 0 else (1 if m < 4 else 2)
                    term = ye[m, k : k + 1, :] * da[m]
                    dv[degree] = term if dv[degree] is None else dv[degree] + term
                    part = da[m] * v[degree]
                    part = part[0:8] + part[8:16] + part[16:24] + part[24:32]
                    at = (m * SLOTS + k) * 8
                    s_acc[at : at + 8, :] += part
                for L in range(3):
                    dq[pl.ds(L * CH + c0, 32), lanes] = (dv[L] * uk).astype(BF16)
                if with_du:
                    total = dv[0] * qk[0] + dv[1] * qk[1] + dv[2] * qk[2]
                    du[pl.ds(c0, 32), lanes] = total.astype(BF16)
            return carry

        lax.fori_loop(0, CH // 32, body, 0)

    def radial_back(layer):
        grad = dot(w4_ref[layer], dq[...])
        for step, ref in ((2, w3_ref), (1, w2_ref), (0, w1_ref)):
            dz = (grad * dsilu[layer, step]).astype(BF16)
            grad = dot(ref[layer], dz)
        return grad

    s_acc[...] = jnp.zeros_like(s_acc)
    radial(0)
    aggregate(0)
    mixed = dot(ow_ref[0], msg[...], TN)
    h1 = (h0 + present * mixed).astype(BF16)
    u1 = dot(up_ref[1], h1, TN).astype(BF16)
    snd2[...] = dot(ps[...], u1, NT).astype(BF16)
    arrived2 = exchange(
        1,
        lambda d: snd2.at[pl.ds(OFF[d], LEN[d])],
        lambda d: rcv2.at[pl.ds(OFF[d], LEN[d])],
    )
    radial(1)
    near = dot(u1, oh[0:SITES, :])
    arrived2()
    u[1] = near + dot(rcv2[...], oh[SITES:EXT, :], TN)
    aggregate(1)
    mixed = dot(ow_ref[1], msg[...], TN)
    h2 = (h1.astype(F32) + present * mixed).astype(BF16)

    diagonal = iota((CH, CH), 0) == iota((CH, CH), 1)
    linear = jnp.sum(jnp.where(diagonal, rl_ref[...], 0.0), axis=1, keepdims=True)
    small = iota((16, 16), 0) == iota((16, 16), 1)
    last = jnp.sum(jnp.where(small, rlast_ref[...], 0.0), axis=1, keepdims=True)
    z = dot(rh_ref[...], h2)
    g, slope_g = silu_parts(z)
    energy = jnp.sum(h1.astype(F32) * linear, axis=0, keepdims=True)
    energy = present * (energy + jnp.sum(g * last, axis=0, keepdims=True))
    dz = (present * last * slope_g).astype(BF16)
    dh2 = dot(rh_ref[...], dz, TN)
    dmixed = (present * dh2).astype(BF16)
    snd_grad = dot(ow_ref[1], dmixed)
    a_grad = mix
    del a_grad
    gs_grad = du
    del gs_grad
    bm = nb
    bm[...] = snd_grad
    aggregate_back(1, bm, True)
    snd3[...] = dot(oh[SITES:EXT, :], du[...], NT).astype(BF16)
    arrived3 = exchange(
        2,
        lambda d: snd3.at[pl.ds(OFF[d], LEN[d])],
        lambda d: rcv3.at[pl.ds(OFF[d], LEN[d])],
    )
    near = dot(du[...], oh[0:SITES, :], NT)
    bessel_grad = radial_back(1)
    arrived3()
    du1 = near + dot(rcv3[...], ps[...], TN)
    dh1 = dh2 + linear * present + dot(up_ref[1], du1.astype(BF16))
    dmixed = (present * dh1).astype(BF16)
    bm[...] = dot(ow_ref[0], dmixed)
    aggregate_back(0, bm, False)
    bessel_grad = bessel_grad + radial_back(0)

    for k in range(SLOTS):
        gs[k * 8 : k * 8 + 8, :] = bessel_grad[:, k * SITES : (k + 1) * SITES]
    dr = rows_of(gs, 0) * bd[0, 0:SLOTS]
    for m in range(1, BES):
        dr = dr + rows_of(gs, m) * bd[m, 0:SLOTS]

    def total_of(m):
        at = m * SLOTS * 8
        out = s_acc[pl.ds(at, SLOTS, stride=8), :]
        for j in range(1, 8):
            out = out + s_acc[pl.ds(at + j, SLOTS, stride=8), :]
        return FACTOR * out

    sums = [total_of(m) for m in range(9)]
    d_env = sums[0]
    for m in range(8):
        d_env = d_env + sums[m + 1] * harmonics[m]
    dr = dr + d_env * slope_w
    dy = [env_w * one for one in sums[1:]]
    dnx = ROOT3 * dy[0] + ROOT15 * (dy[3] * ny + dy[6] * nz + dy[7] * nx)
    dny = ROOT3 * dy[1] + ROOT15 * (dy[3] * nx + dy[4] * nz - dy[7] * ny)
    dnz = ROOT3 * dy[2] + ROOT15 * (dy[4] * ny + dy[6] * nx) + (3.0 * ROOT5) * dy[5] * nz
    radial_part = dr - inv * (dnx * nx + dny * ny + dnz * nz)
    gs[...] = jnp.zeros_like(gs)
    centre = []
    for c, (dn, n) in enumerate(((dnx, nx), (dny, ny), (dnz, nz))):
        dd = dn * inv + radial_part * n
        gs[pl.ds(c, SLOTS, stride=8), :] = dd
        centre.append(jnp.sum(dd, axis=0, keepdims=True))
    edge_grad = jnp.concatenate([gs[k * 8 : k * 8 + 8, :] for k in range(SLOTS)], axis=1)
    scattered = dot(split3(edge_grad), oh[...], NT)
    scattered = scattered[0:8] + scattered[8:16] + scattered[16:24]
    for f in range(2):
        snd4[f] = scattered[:, (f + 1) * SITES : (f + 2) * SITES]
    arrived4 = exchange(3, lambda d: snd4.at[OFF[d] // SITES], lambda d: rcv4.at[d])
    arrived4()
    returned = jnp.concatenate([rcv4[d] for d in range(8)], axis=1)
    back = dot(split3(returned), sel[...], NT)
    back = back[0:8] + back[8:16] + back[16:24] + scattered[:, 0:SITES]

    rows = [jnp.broadcast_to(centre[c] - back[c : c + 1], (16, SITES)) for c in range(3)]
    rows.append(jnp.broadcast_to(energy, (16, SITES)))
    full = jnp.concatenate(rows, axis=0)
    full = jnp.where(yz_mask[0:64], full, 0.0)
    out = dot_exact(full, x_pick, NT)
    for y in range(4):
        for c in range(3):
            force_ref[c, y] = out[c * 16 + y * 4 : c * 16 + y * 4 + 4, 0:8]
        en_ref[y] = out[48 + y * 4 : 52 + y * 4, 0:8]
    for copy in copies:
        copy.wait_send()


def shards(
    positions,
    occupied,
    species,
    neighbours,
    embedding,
    radial_first,
    radial_second,
    radial_third,
    radial_last,
    up_weight,
    product_weight,
    out_weight,
    read_linear,
    read_hidden,
    read_last,
):
    n_gx, n_gy = lax.axis_size("gx"), lax.axis_size("gy")
    vmem = pl.BlockSpec(memory_space=pltpu.VMEM)

    def run(*refs):
        kernel(n_gx, n_gy, *refs)

    energies, forces = pl.pallas_call(
        run,
        out_shape=(
            jax.ShapeDtypeStruct((4, 4, 8), F32),
            jax.ShapeDtypeStruct((3, 4, 4, 8), F32),
        ),
        in_specs=[vmem] * 15,
        out_specs=(vmem, vmem),
        scratch_shapes=[
            pltpu.VMEM((80, SITES), F32),
            pltpu.VMEM((SITES, SITES), F32),
            pltpu.VMEM((8, EXT), F32),
            pltpu.VMEM((SITES, 8 * SITES), BF16),
            pltpu.VMEM((GHOSTS, SITES), BF16),
            pltpu.VMEM((EXT, EDGES), BF16),
            pltpu.VMEM((8, 8, SITES), F32),
            pltpu.VMEM((8, 8, SITES), F32),
            pltpu.VMEM((GHOSTS, CH), BF16),
            pltpu.VMEM((GHOSTS, CH), BF16),
            pltpu.VMEM((GHOSTS, CH), BF16),
            pltpu.VMEM((GHOSTS, CH), BF16),
            pltpu.VMEM((2, 8, SITES), F32),
            pltpu.VMEM((8, 8, SITES), F32),
            pltpu.VMEM((SLOTS * 8, SITES), F32),
            pltpu.VMEM((SLOTS * 8, SITES), F32),
            pltpu.VMEM((9, 16, SITES), F32),
            pltpu.VMEM((BES, 16, SITES), F32),
            pltpu.VMEM((LAYERS, 4, CH, SITES), F32),
            pltpu.VMEM((LAYERS, 3, RAD, EDGES), F32),
            pltpu.VMEM((LAYERS, 3 * CH, EDGES), F32),
            pltpu.VMEM((LAYERS, CH, EDGES), F32),
            pltpu.VMEM((LAYERS, 9, CH, SITES), F32),
            pltpu.VMEM((CH, SITES), BF16),
            pltpu.VMEM((3 * CH, EDGES), BF16),
            pltpu.VMEM((CH, EDGES), BF16),
            pltpu.VMEM((9 * SLOTS * 8, SITES), F32),
            pltpu.SemaphoreType.DMA((4, 8)),
            pltpu.SemaphoreType.DMA((4, 8)),
        ],
        compiler_params=pltpu.CompilerParams(
            collective_id=0, has_side_effects=True, vmem_limit_bytes=48 * 1024 * 1024
        ),
    )(
        positions.transpose(0, 2, 3, 1),
        occupied.transpose(1, 2, 0),
        species.transpose(1, 2, 0),
        neighbours,
        embedding,
        radial_first,
        radial_second,
        radial_third,
        radial_last,
        up_weight,
        product_weight,
        out_weight,
        read_linear,
        read_hidden.T,
        read_last.reshape(1, -1),
    )
    return energies.transpose(2, 0, 1), forces.transpose(0, 3, 1, 2)


def solution(mesh):
    in_specs = (
        P(None, "gx", "gy", None),
        P("gx", "gy", None),
        P("gx", "gy", None),
        P("gx", "gy", None, None),
        P(),
        P(),
        P(),
        P(),
        P(),
        P(),
        P(),
        P(),
        P(),
        P(),
        P(),
    )
    out_specs = (P("gx", "gy", None), P(None, "gx", "gy", None))
    return jax.shard_map(shards, mesh=mesh, in_specs=in_specs, out_specs=out_specs, check_vma=False)
```

profile of v0, /device:TPU:1, one launch (start us, length us, event | category | flops | bytes accessed | tf_op | source)
XLA Modules:
  0.0 71.4 jit_solution(13762689420664278331)
XLA Ops:
  0.6 0.0 copy-start.8
  0.6 0.0 copy-start.13
  0.7 0.0 copy-start.14
  0.7 0.7 copy-done.8
  1.3 0.0 copy-done.13
  1.3 0.0 copy-done.14
  1.3 0.0 copy-start
  1.3 0.9 %copy-done = bf16[2,64,384]{2,1,0:T(8,128)(2,1)S(1)} copy-done((bf16[2,64,384]{2,1,0:T(8,128)(2,1)S(1)}, bf16[2,64,384]{2,1,0:T(8,128)(2,1)}, u32[]{:S(2)}) %copy-start) | copy-done | bytes 98328
  2.2 0.0 copy-start.1
  2.2 0.8 %copy-done.1 = s32[8,4,4,12]{3,2,1,0:T(4,128)S(1)} copy-done((s32[8,4,4,12]{3,2,1,0:T(4,128)S(1)}, s32[8,4,4,12]{3,2,1,0:T(4,128)}, u32[]{:S(2)}) %copy-start.1) | copy-done | bytes 6168
  3.1 0.0 copy-start.2
  3.1 0.8 %copy-done.2 = bf16[2,128,128]{2,1,0:T(8,128)(2,1)S(1)} copy-done((bf16[2,128,128]{2,1,0:T(8,128)(2,1)S(1)}, bf16[2,128,128]{2,1,0:T(8,128)(2,1)}, u32[]{:S(2)}) %copy-start.2) | copy-done | bytes 65560
  3.9 0.0 copy-start.3
  3.9 0.8 %copy-done.3 = bf16[2,128,128]{2,1,0:T(8,128)(2,1)S(1)} copy-done((bf16[2,128,128]{2,1,0:T(8,128)(2,1)S(1)}, bf16[2,128,128]{2,1,0:T(8,128)(2,1)}, u32[]{:S(2)}) %copy-start.3) | copy-done | bytes 65560
  4.8 0.0 copy-start.4
  4.8 0.8 %copy-done.4 = f32[2,10,4,128]{3,2,1,0:T(4,128)S(1)} copy-done((f32[2,10,4,128]{3,2,1,0:T(4,128)S(1)}, f32[2,10,4,128]{3,2,1,0:T(4,128)}, u32[]{:S(2)}) %copy-start.4) | copy-done | bytes 40984
  5.5 0.0 copy-start.5
  5.5 0.8 %copy-done.5 = bf16[2,64,64]{2,1,0:T(8,128)(2,1)S(1)} copy-done((bf16[2,64,64]{2,1,0:T(8,128)(2,1)S(1)}, bf16[2,64,64]{2,1,0:T(8,128)(2,1)}, u32[]{:S(2)}) %copy-start.5) | copy-done | bytes 16408
  6.3 0.0 copy-start.6
  6.3 0.8 %copy-done.6 = bf16[2,64,64]{2,1,0:T(8,128)(2,1)S(1)} copy-done((bf16[2,64,64]{2,1,0:T(8,128)(2,1)S(1)}, bf16[2,64,64]{2,1,0:T(8,128)(2,1)}, u32[]{:S(2)}) %copy-start.6) | copy-done | bytes 16408
  7.0 0.0 copy-start.7
  7.1 0.7 %copy-done.7 = f32[3,8,4,4]{1,3,2,0:T(4,128)S(1)} copy-done((f32[3,8,4,4]{1,3,2,0:T(4,128)S(1)}, f32[3,8,4,4]{1,3,2,0:T(4,128)}, u32[]{:S(2)}) %copy-start.7) | copy-done | bytes 1560
  7.8 0.0 copy-start.9
  7.8 0.7 copy-done.9
  8.5 0.7 copy-done.10
  9.2 0.0 copy-start.11
  9.2 0.7 copy-done.11
  9.9 0.0 copy-start.12
  9.9 0.7 copy-done.12
  10.5 59.7 %shard_map.158 = (f32[4,4,8]{2,1,0:T(4,128)S(1)}, f32[3,4,4,8]{3,2,1,0:T(4,128)S(1)}) custom-call(f32[3,4,4,8]{3,2,1,0:T(4,128)S(1)} %bitcast.7, s32[4,4,8]{2,1,0:T(4,128)S(1)} %bitcast.9, s32[4,4,8]{2,1,0:T(4,128)S(1)} %bitcast.10, s32[8,4,4,12]{3,2,1,0:T(4,128)S(1)} %copy-done.1, bf16[10,128]{1,0:T(8,128)(2,1)S(1)} %copy-done.10, ...), custom_call_target="tpu_custom_call" | custom-call | tf_op jit(solution)/shard_map/pallas_call | solution.py:502
  70.2 0.6 copy.19
  70.8 0.6 copy.20
  (1 shorter events, 0.0 us)
Async XLA Ops:
  0.6 0.7 copy-start.8
  0.6 0.7 copy-start.13
  0.7 0.7 copy-start.14
  1.3 0.9 %copy-start = (bf16[2,64,384]{2,1,0:T(8,128)(2,1)S(1)}, bf16[2,64,384]{2,1,0:T(8,128)(2,1)}, u32[]{:S(2)}) copy-start(bf16[2,64,384]{2,1,0:T(8,128)(2,1)} %refs_8_.1) | copy-start | bytes 294916
  2.2 0.8 %copy-start.1 = (s32[8,4,4,12]{3,2,1,0:T(4,128)S(1)}, s32[8,4,4,12]{3,2,1,0:T(4,128)}, u32[]{:S(2)}) copy-start(s32[8,4,4,12]{3,2,1,0:T(4,128)} %refs_3_.1) | copy-start | bytes 18436
  3.1 0.8 %copy-start.2 = (bf16[2,128,128]{2,1,0:T(8,128)(2,1)S(1)}, bf16[2,128,128]{2,1,0:T(8,128)(2,1)}, u32[]{:S(2)}) copy-start(bf16[2,128,128]{2,1,0:T(8,128)(2,1)} %refs_9_.1) | copy-start | bytes 196612
  3.9 0.8 %copy-start.3 = (bf16[2,128,128]{2,1,0:T(8,128)(2,1)S(1)}, bf16[2,128,128]{2,1,0:T(8,128)(2,1)}, u32[]{:S(2)}) copy-start(bf16[2,128,128]{2,1,0:T(8,128)(2,1)} %refs_11_.1) | copy-start | bytes 196612
  4.8 0.8 %copy-start.4 = (f32[2,10,4,128]{3,2,1,0:T(4,128)S(1)}, f32[2,10,4,128]{3,2,1,0:T(4,128)}, u32[]{:S(2)}) copy-start(f32[2,10,4,128]{3,2,1,0:T(4,128)} %refs_10_.1) | copy-start | bytes 122884
  5.5 0.8 %copy-start.5 = (bf16[2,64,64]{2,1,0:T(8,128)(2,1)S(1)}, bf16[2,64,64]{2,1,0:T(8,128)(2,1)}, u32[]{:S(2)}) copy-start(bf16[2,64,64]{2,1,0:T(8,128)(2,1)} %refs_6_.1) | copy-start | bytes 49156
  6.3 0.8 %copy-start.6 = (bf16[2,64,64]{2,1,0:T(8,128)(2,1)S(1)}, bf16[2,64,64]{2,1,0:T(8,128)(2,1)}, u32[]{:S(2)}) copy-start(bf16[2,64,64]{2,1,0:T(8,128)(2,1)} %refs_7_.1) | copy-start | bytes 49156
  7.0 0.7 %copy-start.7 = (f32[3,8,4,4]{1,3,2,0:T(4,128)S(1)}, f32[3,8,4,4]{1,3,2,0:T(4,128)}, u32[]{:S(2)}) copy-start(f32[3,8,4,4]{1,3,2,0:T(4,128)} %param.15) | copy-start | bytes 4612
  7.8 0.7 copy-start.9
  8.5 0.7 copy-start.10
  9.2 0.7 copy-start.11
  9.9 0.7 copy-start.12
where the time goes:
time: 72.2 us; the launch traced here: 71.4 us
  Pallas kernels  59.7 us (83%)
  local copies, waits for them, and re-layouts  11.1 us (15%)
    pallas_call x1, Pallas kernels, shards(): pl.pallas_call(run, out_shape=(jax.ShapeDtypeStruct((4, 4, 8), F32), jax....  59.7 us
    unnamed x32, local copies, waits for them, and re-layouts  11.1 us

commit v1 on v0

v1 whole, which is shorter than its diff:
```python
import functools
import math

import jax
import jax.numpy as jnp
from jax import lax
from jax.experimental import pallas as pl
from jax.experimental.pallas import tpu as pltpu
from jax.sharding import PartitionSpec as P

F32 = jnp.float32
BF16 = jnp.bfloat16
MESH = pl.DeviceIdType.MESH
CUTOFF = 5.0
SLOTS = 12
SITES = 128
EDGES = SITES * SLOTS
GHOSTS = 304
EXT = SITES + GHOSTS
CH = 128
RAD = 64
BES = 8
LAYERS = 2

LEFT, RIGHT, ACROSS = 128, 256, 384

NT = (((1,), (1,)), ((), ()))
TN = (((0,), (0,)), ((), ()))
NN = (((1,), (0,)), ((), ()))


def dot(a, b, dims=NN):
    return lax.dot_general(a, b, dims, preferred_element_type=F32)


def dot_exact(a, b, dims=NN):
    return lax.dot_general(a, b, dims, preferred_element_type=F32, precision=lax.Precision.HIGHEST)


def iota(shape, dim):
    return lax.broadcasted_iota(jnp.int32, shape, dim)


def split3(x):
    high = x.astype(BF16).astype(F32)
    rest = x - high
    middle = rest.astype(BF16).astype(F32)
    return jnp.concatenate([high, middle, rest - middle], axis=0).astype(BF16)


def split2(x):
    high = x.astype(BF16).astype(F32)
    return jnp.concatenate([high, x - high], axis=0).astype(BF16)


def silu_parts(z):
    s = 0.5 + 0.5 * jnp.tanh(0.5 * z)
    g = z * s
    return g, s + g * (1.0 - s)


ROOT3 = math.sqrt(3.0)
ROOT5 = math.sqrt(5.0)
ROOT15 = math.sqrt(15.0)
FACTOR = 1.0 / math.sqrt(SLOTS)


def kernel(n_gx, *refs):
    inputs, refs = refs[:15], refs[15:]
    (en_ref, force_ref), refs = refs[:2], refs[2:]
    held, refs = refs[:15], refs[15:]
    (raw, nb, tile, geo, ps, oh, rcv1, snd2, rcv2, snd3, rcv3, snd4, rcv4), refs = refs[:13], refs[13:]
    (gs, bs, ye, bd, mix, dsilu, q, u, a, msg, dq, du, s_acc), refs = refs[:13], refs[13:]
    fetch_sem, send_sem, recv_sem = refs
    (pos_ref, occ_ref, spec_ref, nbr_ref, emb_ref, w1_ref, w2_ref, w3_ref, w4_ref), more = held[:9], held[9:]
    up_ref, pw_ref, ow_ref, rl_ref, rh_ref, rlast_ref = more

    fetches = []
    for i in range(15):
        fetch = pltpu.make_async_copy(inputs[i], held[i], fetch_sem.at[i])
        fetch.start()
        fetches.append(fetch)

    gx = lax.axis_index("gx")
    gy = lax.axis_index("gy")
    j, c = gy // 2, gy % 2
    own_half, own_slot = gy // 4, gy % 4
    edge = (gy == 3) | (gy == 4)
    halo_gy = 4 - c
    first, last_gx = gx == 0, gx == n_gx - 1
    has_left = jnp.logical_not((j == 0) & first)
    has_right = jnp.logical_not((j == 3) & last_gx)
    has_other = ((j == 0) | (j == 3)) & has_left & has_right
    other_gx = jnp.where(j == 0, gx - 1, gx + 1)
    left = (jnp.where(j == 0, gx - 1, gx), jnp.where(j == 0, 6, 2 * j - 2))
    right = (jnp.where(j == 3, gx + 1, gx), jnp.where(j == 3, 0, 2 * j + 2))
    always = gx >= 0
    regions = (
        (has_left, (left[0], left[1] + c), 0, 128),
        (has_right, (right[0], right[1] + c), 128, 128),
        (always, (gx, 2 * j + 1 - c), 256, 16),
        (has_left, (left[0], left[1] + 1 - c), 272, 16),
        (has_right, (right[0], right[1] + 1 - c), 288, 16),
    )
    facing = (1, 0, 2, 4, 3)
    owners = []
    for group in range(2):
        for m in range(5):
            owner_gy = 4 * c + m if m < 4 else halo_gy
            if group == 0:
                owners.append((owner_gy != gy, owner_gy == gy, (gx, owner_gy)))
            else:
                owners.append((has_other, None, (other_gx, owner_gy)))
    readers = []
    for side in range(2):
        half = own_half if side == 0 else 1 - own_half
        slot = own_slot if side == 0 else 4
        wanted = always if side == 0 else edge
        for p in range(4):
            here = 2 * p + half == gy
            readers.append((wanted & jnp.logical_not(here), wanted & here, (gx, 2 * p + half), slot))
        readers.append((wanted & jnp.logical_not(first), None, (gx - 1, 6 + half), slot + 5))
        readers.append((wanted & jnp.logical_not(last_gx), None, (gx + 1, half), slot + 5))

    rcv1[...] = jnp.zeros_like(rcv1)
    rcv2[...] = jnp.zeros_like(rcv2)
    rcv3[...] = jnp.zeros_like(rcv3)
    rcv4[...] = jnp.zeros_like(rcv4)
    barrier = pltpu.get_barrier_semaphore()

    def greet(there, device):
        @pl.when(there)
        def _():
            pl.semaphore_signal(barrier, inc=1, device_id=device, device_id_type=MESH)

    for there, _, device in owners:
        greet(there, device)
    for there, device, _, _ in regions:
        greet(there, device)
    greetings = jnp.int32(0)
    for there, _, _, _ in readers + list(regions):
        greetings = greetings + there.astype(jnp.int32)

    sent = []

    def send(there, here, device, source, target, phase, at, slot):
        def remote():
            return pltpu.make_async_remote_copy(
                src_ref=source,
                dst_ref=target,
                send_sem=send_sem.at[phase, at],
                recv_sem=recv_sem.at[phase, slot],
                device_id=device,
                device_id_type=MESH,
            )

        @pl.when(there)
        def _():
            remote().start()

        if here is not None:

            @pl.when(here)
            def _():
                pltpu.make_async_copy(source, target, recv_sem.at[phase, slot]).start()

        sent.append((there, remote))

    def receive(there, target, phase, slot):
        @pl.when(there)
        def _():
            pltpu.make_async_copy(target, target, recv_sem.at[phase, slot]).wait()

    raw[...] = jnp.zeros_like(raw)
    nb[...] = jnp.zeros_like(nb)
    tile[...] = jnp.zeros_like(tile)
    x_pick = (iota((SITES, SITES), 0) == iota((SITES, SITES), 1) // 16).astype(F32)
    yz_mask = iota((80, SITES), 0) % 16 == iota((80, SITES), 1) % 16
    for i in range(4):
        fetches[i].wait()
    for y in range(4):
        for axis in range(3):
            raw[axis * 16 + y * 4 : axis * 16 + y * 4 + 4, 0:8] = pos_ref[axis, y]
        raw[48 + y * 4 : 52 + y * 4, 0:8] = occ_ref[y].astype(F32)
        raw[64 + y * 4 : 68 + y * 4, 0:8] = spec_ref[y].astype(F32)
    for x in range(8):
        for y in range(4):
            nb[x * 16 + y * 4 : x * 16 + y * 4 + 4, 0:SLOTS] = nbr_ref[x, y].astype(F32)
    spread = jnp.where(yz_mask, dot_exact(raw[...], x_pick), 0.0)
    for f in range(5):
        tile[f : f + 1, :] = jnp.sum(spread[f * 16 : f * 16 + 16], axis=0, keepdims=True)
    tile[8:24, :] = nb[...].T[0:16]

    pl.semaphore_wait(barrier, greetings)
    for at, (there, here, device, slot) in enumerate(readers):
        rows = 24 if at < 4 else 8
        send(there, here, device, tile.at[0:rows], rcv1.at[slot, 0:rows], 0, at, slot)

    rows = iota((GHOSTS, SITES), 0)
    y_strip = 14 * (1 - c)
    strip = rows % 16 // 8 * 64 + (y_strip + rows % 8 // 4) * 4 + rows % 4
    hit = jnp.where(rows < 256, rows % 128, strip) == iota((GHOSTS, SITES), 1)
    ps[...] = jnp.where(hit, 1.0, 0.0).astype(BF16)
    for i in range(4, 15):
        fetches[i].wait()
    lifted_table = dot(emb_ref[...], up_ref[0]).astype(BF16).astype(F32)
    s_acc[...] = jnp.zeros_like(s_acc)
    geo[...] = jnp.zeros_like(geo)

    for slot in range(10):
        rows = 24 if slot < 4 else 8
        receive(always if slot < 5 else has_other, rcv1.at[slot, 0:rows], 0, slot)

    lane = iota((8, SITES), 1)
    no = gx < 0
    slabs = (
        (2 * j, no),
        (jnp.where(j == 0, 6, 2 * j - 2), j == 0),
        (jnp.where(j == 3, 0, 2 * j + 2), j == 3),
    )
    y_halo = 2 * c

    def slab_shift(x0, m, x):
        return lax.rem(2 * SITES + x * 64 + m * 16 - (x0 + x) * 16, SITES)

    def strip_shift(x0, r, x):
        return lax.rem(2 * SITES + r * 16 + x * 8 - (x0 + x) * 16 - y_halo * 4, SITES)

    for r, (x0, other) in enumerate(slabs):
        out = jnp.zeros((8, SITES), F32)
        for m in range(4):
            source = rcv1[m, 0:8]
            if r > 0:
                source = jnp.where(other, rcv1[5 + m, 0:8], source)
            for x in range(2):
                moved = pltpu.roll(source, slab_shift(x0, m, x), 1)
                out = jnp.where(lane // 16 == x * 4 + m, moved, out)
        geo[:, r * SITES : (r + 1) * SITES] = out
    out = jnp.zeros((8, SITES), F32)
    for r, (x0, other) in enumerate(slabs):
        source = rcv1[4, 0:8]
        if r > 0:
            source = jnp.where(other, rcv1[9, 0:8], source)
        for x in range(2):
            moved = pltpu.roll(source, strip_shift(x0, r, x), 1)
            out = jnp.where(lane // 8 == r * 2 + x, moved, out)
    geo[:, 3 * SITES : 4 * SITES] = out

    lane16 = iota((16, SITES), 1)
    index = jnp.zeros((16, SITES), F32)
    for m in range(4):
        for x in range(2):
            moved = pltpu.roll(rcv1[m, 8:24], slab_shift(2 * j, m, x), 1)
            index = jnp.where(lane16 // 16 == x * 4 + m, moved, index)
    index = index.astype(jnp.int32)
    z = index & 3
    y = ((index >> 2) & 7) - 2 + lane16 // 16 % 4 * 4
    x = (index >> 5) - 2 - 2 * j
    inner = (x & 1) * 64 + y * 4 + z + jnp.where(x < 0, LEFT, jnp.where(x > 1, RIGHT, 0))
    outer = (x & 1) * 8 + (y & 1) * 4 + z + jnp.where(x < 0, ACROSS + 16, jnp.where(x > 1, ACROSS + 32, ACROSS))
    beyond = jnp.where(c == 0, y - 16, -1 - y) >= 0
    place = jnp.where((y >= 0) & (y < 16), inner, jnp.where(beyond, outer, -1))
    ext_row = iota((EXT, SITES), 0)
    for k in range(SLOTS):
        hit = ext_row == place[k : k + 1]
        oh[:, k * SITES : (k + 1) * SITES] = jnp.where(hit, 1.0, 0.0).astype(BF16)

    gathered = dot(split3(geo[:, 0:EXT]), oh[...])
    gathered = gathered[0:8] + gathered[8:16] + gathered[16:24]
    for k in range(SLOTS):
        gs[k * 8 : k * 8 + 8, :] = gathered[:, k * SITES : (k + 1) * SITES]
    ext_hot = (geo[4:5, 0:EXT].astype(jnp.int32) == iota((16, EXT), 0)).astype(F32)
    u0 = dot(lifted_table, ext_hot[0:10], TN).astype(BF16)
    u[0] = dot(u0, oh[...])

    present = geo[3:4, 0:SITES]
    own_hot = ext_hot[:, 0:SITES]
    for layer in range(LAYERS):
        for k in range(4):
            mix[layer, k] = dot_exact(pw_ref[layer, :, k, :], own_hot[0:10], TN)
    h0 = dot(emb_ref[...].astype(F32), own_hot[0:10], TN) * present

    def rows_of(ref, m):
        return ref[pl.ds(m, SLOTS, stride=8), :]

    disp = [rows_of(gs, c) - geo[c : c + 1, 0:SITES] for c in range(3)]
    w = rows_of(gs, 3) * present
    squared = disp[0] * disp[0] + disp[1] * disp[1] + disp[2] * disp[2]
    dist = jnp.sqrt(jnp.where(w > 0, squared, 1.0))
    inv = 1.0 / dist
    nx, ny, nz = [c * inv for c in disp]
    scaled = jnp.minimum(dist * (1.0 / CUTOFF), 1.0)
    u2 = scaled * scaled
    u5 = u2 * u2 * scaled
    u6 = u5 * scaled
    env = 1.0 - 28.0 * u6 + 48.0 * u6 * scaled - 21.0 * u6 * u2
    env = jnp.where(scaled < 1.0, env, 0.0)
    gap = 1.0 - scaled
    slope = (-168.0 / CUTOFF) * u5 * gap * gap
    env_w = env * w
    slope_w = slope * w
    ye_scale = FACTOR * env_w
    harmonics = [
        ROOT3 * nx,
        ROOT3 * ny,
        ROOT3 * nz,
        ROOT15 * nx * ny,
        ROOT15 * ny * nz,
        0.5 * ROOT5 * (3.0 * nz * nz - 1.0),
        ROOT15 * nx * nz,
        0.5 * ROOT15 * (nx * nx - ny * ny),
    ]
    ye[0, 0:SLOTS] = ye_scale
    for m in range(8):
        ye[m + 1, 0:SLOTS] = ye_scale * harmonics[m]
    theta = math.pi * scaled
    sin1 = jnp.sin(theta)
    cos1 = jnp.cos(theta)
    twice = 2.0 * cos1
    sin_before, cos_before = jnp.zeros_like(sin1), jnp.ones_like(cos1)
    sin_m, cos_m = sin1, cos1
    amplitude = math.sqrt(2.0 / CUTOFF) * inv
    for m in range(BES):
        value = amplitude * sin_m
        bs[pl.ds(m, SLOTS, stride=8), :] = value
        bd[m, 0:SLOTS] = amplitude * ((m + 1) * math.pi / CUTOFF) * cos_m - value * inv
        sin_m, sin_before = twice * sin_m - sin_before, sin_m
        cos_m, cos_before = twice * cos_m - cos_before, cos_m

    def radial(layer):
        hidden = jnp.concatenate([bs[k * 8 : k * 8 + 8, :] for k in range(SLOTS)], axis=1)
        hidden = hidden.astype(BF16)
        for step, ref in enumerate((w1_ref, w2_ref, w3_ref)):
            z = dot(ref[layer], hidden, TN)
            g, slope_g = silu_parts(z)
            dsilu[layer, step] = slope_g
            hidden = g.astype(BF16)
        q[layer] = dot(w4_ref[layer], hidden, TN)

    def aggregate(layer):
        def body(block, carry):
            c0 = pl.multiple_of(block * 32, 32)
            acc = [jnp.zeros((32, SITES), F32) for _ in range(9)]
            for k in range(SLOTS):
                lanes = slice(k * SITES, (k + 1) * SITES)
                uk = u[layer, pl.ds(c0, 32), lanes]
                v = [q[layer, pl.ds(L * CH + c0, 32), lanes] * uk for L in range(3)]
                for m in range(9):
                    degree = 0 if m == 0 else (1 if m < 4 else 2)
                    acc[m] = acc[m] + ye[m, k : k + 1, :] * v[degree]
            for m in range(9):
                a[layer, m, pl.ds(c0, 32), :] = acc[m]
            p = [mix[layer, j, pl.ds(c0, 32), :] for j in range(4)]
            first = acc[1] * acc[1] + acc[2] * acc[2] + acc[3] * acc[3]
            second = acc[4] * acc[4] + acc[5] * acc[5] + acc[6] * acc[6]
            second = second + acc[7] * acc[7] + acc[8] * acc[8]
            result = p[0] * acc[0] + p[1] * acc[0] * acc[0] + p[2] * first + p[3] * second
            msg[pl.ds(c0, 32), :] = result.astype(BF16)
            return carry

        lax.fori_loop(0, CH // 32, body, 0)

    def aggregate_back(layer, msg_grad_ref, with_du):
        def body(block, carry):
            c0 = pl.multiple_of(block * 32, 32)
            g = msg_grad_ref[pl.ds(c0, 32), :]
            p = [mix[layer, j, pl.ds(c0, 32), :] for j in range(4)]
            a0 = a[layer, 0, pl.ds(c0, 32), :]
            scale1 = 2.0 * p[2] * g
            scale2 = 2.0 * p[3] * g
            da = [g * (p[0] + 2.0 * p[1] * a0)]
            for m in range(1, 9):
                da.append((scale1 if m < 4 else scale2) * a[layer, m, pl.ds(c0, 32), :])
            for k in range(SLOTS):
                lanes = slice(k * SITES, (k + 1) * SITES)
                uk = u[layer, pl.ds(c0, 32), lanes]
                qk = [q[layer, pl.ds(L * CH + c0, 32), lanes] for L in range(3)]
                v = [one * uk for one in qk]
                dv = [None, None, None]
                for m in range(9):
                    degree = 0 if m == 0 else (1 if m < 4 else 2)
                    term = ye[m, k : k + 1, :] * da[m]
                    dv[degree] = term if dv[degree] is None else dv[degree] + term
                    part = da[m] * v[degree]
                    part = part[0:8] + part[8:16] + part[16:24] + part[24:32]
                    at = (m * SLOTS + k) * 8
                    s_acc[at : at + 8, :] += part
                for L in range(3):
                    dq[pl.ds(L * CH + c0, 32), lanes] = (dv[L] * uk).astype(BF16)
                if with_du:
                    total = dv[0] * qk[0] + dv[1] * qk[1] + dv[2] * qk[2]
                    du[pl.ds(c0, 32), lanes] = total.astype(BF16)
            return carry

        lax.fori_loop(0, CH // 32, body, 0)

    def radial_back(layer):
        grad = dot(w4_ref[layer], dq[...])
        for step, ref in ((2, w3_ref), (1, w2_ref), (0, w1_ref)):
            dz = (grad * dsilu[layer, step]).astype(BF16)
            grad = dot(ref[layer], dz)
        return grad

    radial(0)
    aggregate(0)
    mixed = dot(ow_ref[0], msg[...], TN)
    h1 = (h0 + present * mixed).astype(BF16)
    u1 = dot(up_ref[1], h1, TN).astype(BF16)
    snd2[...] = dot(ps[128:272, :], u1, NT).astype(BF16)
    for r, (there, device, start, size) in enumerate(regions):
        source = snd2.at[0:128] if r < 2 else snd2.at[128:144]
        start = regions[facing[r]][2]
        send(there, None, device, source, rcv2.at[start : start + size], 1, r, facing[r])
    radial(1)
    near = dot(u1, oh[0:SITES, :])
    for r, (there, _, start, size) in enumerate(regions):
        receive(there, rcv2.at[start : start + size], 1, r)
    u[1] = near + dot(rcv2[...], oh[SITES:EXT, :], TN)
    aggregate(1)
    mixed = dot(ow_ref[1], msg[...], TN)
    h2 = (h1.astype(F32) + present * mixed).astype(BF16)

    diagonal = iota((CH, CH), 0) == iota((CH, CH), 1)
    linear = jnp.sum(jnp.where(diagonal, rl_ref[...], 0.0), axis=1, keepdims=True)
    small = iota((16, 16), 0) == iota((16, 16), 1)
    last = jnp.sum(jnp.where(small, rlast_ref[...], 0.0), axis=1, keepdims=True)
    z = dot(rh_ref[...], h2)
    g, slope_g = silu_parts(z)
    energy = jnp.sum(h1.astype(F32) * linear, axis=0, keepdims=True)
    energy = present * (energy + jnp.sum(g * last, axis=0, keepdims=True))
    dz = (present * last * slope_g).astype(BF16)
    dh2 = dot(rh_ref[...], dz, TN)
    dmixed = (present * dh2).astype(BF16)
    message_grad = dot(ow_ref[1], dmixed)
    bm = nb
    bm[...] = message_grad
    aggregate_back(1, bm, True)
    snd3[...] = dot(oh[SITES:EXT, :], du[...], NT).astype(BF16)
    for r, (there, device, start, size) in enumerate(regions):
        target = regions[facing[r]][2]
        source = snd3.at[start : start + size]
        send(there, None, device, source, rcv3.at[target : target + size], 2, r, facing[r])
    near = dot(du[...], oh[0:SITES, :], NT)
    bessel_grad = radial_back(1)
    for r, (there, _, start, size) in enumerate(regions):
        receive(there, rcv3.at[start : start + size], 2, r)
    du1 = near + dot(rcv3[...], ps[...], TN)
    dh1 = dh2 + linear * present + dot(up_ref[1], du1.astype(BF16))
    dmixed = (present * dh1).astype(BF16)
    bm[...] = dot(ow_ref[0], dmixed)
    aggregate_back(0, bm, False)
    bessel_grad = bessel_grad + radial_back(0)

    for k in range(SLOTS):
        gs[k * 8 : k * 8 + 8, :] = bessel_grad[:, k * SITES : (k + 1) * SITES]
    dr = rows_of(gs, 0) * bd[0, 0:SLOTS]
    for m in range(1, BES):
        dr = dr + rows_of(gs, m) * bd[m, 0:SLOTS]

    def total_of(m):
        at = m * SLOTS * 8
        out = s_acc[pl.ds(at, SLOTS, stride=8), :]
        for j in range(1, 8):
            out = out + s_acc[pl.ds(at + j, SLOTS, stride=8), :]
        return FACTOR * out

    sums = [total_of(m) for m in range(9)]
    d_env = sums[0]
    for m in range(8):
        d_env = d_env + sums[m + 1] * harmonics[m]
    dr = dr + d_env * slope_w
    dy = [env_w * one for one in sums[1:]]
    dnx = ROOT3 * dy[0] + ROOT15 * (dy[3] * ny + dy[6] * nz + dy[7] * nx)
    dny = ROOT3 * dy[1] + ROOT15 * (dy[3] * nx + dy[4] * nz - dy[7] * ny)
    dnz = ROOT3 * dy[2] + ROOT15 * (dy[4] * ny + dy[6] * nx) + (3.0 * ROOT5) * dy[5] * nz
    radial_part = dr - inv * (dnx * nx + dny * ny + dnz * nz)
    gs[...] = jnp.zeros_like(gs)
    centre = []
    for axis, (dn, n) in enumerate(((dnx, nx), (dny, ny), (dnz, nz))):
        dd = dn * inv + radial_part * n
        gs[pl.ds(axis, SLOTS, stride=8), :] = dd
        centre.append(jnp.sum(dd, axis=0, keepdims=True))
    edge_grad = jnp.concatenate([gs[k * 8 : k * 8 + 8, :] for k in range(SLOTS)], axis=1)
    scattered = dot(split3(edge_grad), oh[...], NT)
    geo[:, 0:EXT] = scattered[0:8] + scattered[8:16] + scattered[16:24]
    for axis in range(3):
        geo[axis : axis + 1, 0:SITES] = geo[axis : axis + 1, 0:SITES] - centre[axis]
    geo[3:4, 0:SITES] = energy

    for m in range(4):
        tiles = [jnp.zeros((8, SITES), F32) for _ in range(2)]
        for r, (x0, other) in enumerate(slabs):
            for x in range(2):
                moved = pltpu.roll(geo[:, r * SITES : (r + 1) * SITES], lax.rem(SITES - slab_shift(x0, m, x), SITES), 1)
                tiles[0] = jnp.where(lane // 16 == jnp.where(other, -1, x0 + x), moved, tiles[0])
                if r > 0:
                    tiles[1] = jnp.where(lane // 16 == jnp.where(other, x0 + x, -1), moved, tiles[1])
        snd4[m] = tiles[0]
        snd4[5 + m] = tiles[1]
    tiles = [jnp.zeros((8, SITES), F32) for _ in range(2)]
    for r, (x0, other) in enumerate(slabs):
        for x in range(2):
            moved = pltpu.roll(geo[:, 3 * SITES :], lax.rem(SITES - strip_shift(x0, r, x), SITES), 1)
            at = 2 * (x0 + x) + c
            tiles[0] = jnp.where(lane // 8 == jnp.where(other, -1, at), moved, tiles[0])
            tiles[1] = jnp.where(lane // 8 == jnp.where(other, at, -1), moved, tiles[1])
    snd4[4] = tiles[0]
    snd4[9] = tiles[1]
    for at, (there, here, device) in enumerate(owners):
        slot = j if at < 5 else jnp.where(j == 0, 5, 4)
        slot = slot + (6 if at % 5 == 4 else 0)
        send(there, here, device, snd4.at[at], rcv4.at[slot], 3, at, slot)
    for at, (there, here, _, _) in enumerate(readers):
        wanted = there if here is None else there | here
        receive(wanted, rcv4.at[at], 3, at)
    back = rcv4[0]
    for at in range(1, 12):
        back = back + rcv4[at]

    rows = [jnp.broadcast_to(-back[axis : axis + 1], (16, SITES)) for axis in range(3)]
    rows.append(jnp.broadcast_to(back[3:4], (16, SITES)))
    full = jnp.where(yz_mask[0:64], jnp.concatenate(rows, axis=0), 0.0)
    out = dot_exact(full, x_pick, NT)
    for y in range(4):
        for axis in range(3):
            force_ref[axis, y] = out[axis * 16 + y * 4 : axis * 16 + y * 4 + 4, 0:8]
        en_ref[y] = out[48 + y * 4 : 52 + y * 4, 0:8]
    for there, remote in sent:

        @pl.when(there)
        def _():
            remote().wait_send()


def shards(
    positions,
    occupied,
    species,
    neighbours,
    embedding,
    radial_first,
    radial_second,
    radial_third,
    radial_last,
    up_weight,
    product_weight,
    out_weight,
    read_linear,
    read_hidden,
    read_last,
):
    n_gx = lax.axis_size("gx")
    vmem = pl.BlockSpec(memory_space=pltpu.VMEM)
    operands = (
        positions.transpose(0, 2, 3, 1),
        occupied.transpose(1, 2, 0),
        species.transpose(1, 2, 0),
        neighbours,
        embedding,
        radial_first,
        radial_second,
        radial_third,
        radial_last,
        up_weight,
        product_weight,
        out_weight,
        read_linear,
        read_hidden.T,
        read_last.reshape(1, -1),
    )
    energies, forces = pl.pallas_call(
        functools.partial(kernel, n_gx),
        out_shape=(
            jax.ShapeDtypeStruct((4, 4, 8), F32),
            jax.ShapeDtypeStruct((3, 4, 4, 8), F32),
        ),
        in_specs=[pl.BlockSpec(memory_space=pltpu.HBM)] * 15,
        out_specs=(vmem, vmem),
        scratch_shapes=[pltpu.VMEM(one.shape, one.dtype) for one in operands]
        + [
            pltpu.VMEM((80, SITES), F32),
            pltpu.VMEM((SITES, SITES), F32),
            pltpu.VMEM((24, SITES), F32),
            pltpu.VMEM((8, 4 * SITES), F32),
            pltpu.VMEM((GHOSTS, SITES), BF16),
            pltpu.VMEM((EXT, EDGES), BF16),
            pltpu.VMEM((10, 24, SITES), F32),
            pltpu.VMEM((144, CH), BF16),
            pltpu.VMEM((GHOSTS, CH), BF16),
            pltpu.VMEM((GHOSTS, CH), BF16),
            pltpu.VMEM((GHOSTS, CH), BF16),
            pltpu.VMEM((10, 8, SITES), F32),
            pltpu.VMEM((12, 8, SITES), F32),
            pltpu.VMEM((SLOTS * 8, SITES), F32),
            pltpu.VMEM((SLOTS * 8, SITES), F32),
            pltpu.VMEM((9, 16, SITES), F32),
            pltpu.VMEM((BES, 16, SITES), F32),
            pltpu.VMEM((LAYERS, 4, CH, SITES), F32),
            pltpu.VMEM((LAYERS, 3, RAD, EDGES), F32),
            pltpu.VMEM((LAYERS, 3 * CH, EDGES), F32),
            pltpu.VMEM((LAYERS, CH, EDGES), F32),
            pltpu.VMEM((LAYERS, 9, CH, SITES), F32),
            pltpu.VMEM((CH, SITES), BF16),
            pltpu.VMEM((3 * CH, EDGES), BF16),
            pltpu.VMEM((CH, EDGES), BF16),
            pltpu.VMEM((9 * SLOTS * 8, SITES), F32),
            pltpu.SemaphoreType.DMA((15,)),
            pltpu.SemaphoreType.DMA((4, 12)),
            pltpu.SemaphoreType.DMA((4, 12)),
        ],
        compiler_params=pltpu.CompilerParams(
            collective_id=0, has_side_effects=True, vmem_limit_bytes=60 * 1024 * 1024
        ),
    )(*operands)
    return energies.transpose(2, 0, 1), forces.transpose(0, 3, 1, 2)


def solution(mesh):
    in_specs = (
        P(None, "gx", "gy", None),
        P("gx", "gy", None),
        P("gx", "gy", None),
        P("gx", "gy", None, None),
        P(),
        P(),
        P(),
        P(),
        P(),
        P(),
        P(),
        P(),
        P(),
        P(),
        P(),
    )
    out_specs = (P("gx", "gy", None), P(None, "gx", "gy", None))
    return jax.shard_map(shards, mesh=mesh, in_specs=in_specs, out_specs=out_specs, check_vma=False)
```

time: 72.2 us -> 51.6 us (0.71)
  the two profiles are of different devices: /device:TPU:1 before, /device:TPU:7 now
where the time goes in v1:
time: 51.6 us; the launch traced here: 51.4 us
  Pallas kernels  48.1 us (93%)
  local copies, waits for them, and re-layouts  2.64 us (5%)
  between operations  0.64 us (1%)
    pallas_call x1, Pallas kernels, shards(): pl.pallas_call(functools.partial(kernel, n_gx), out_shape=(jax.ShapeDtype...  48.1 us
    unnamed x2, local copies, waits for them, and re-layouts  2.64 us

profile of v1, /device:TPU:7, one launch (start us, length us, event | category | flops | bytes accessed | tf_op | source)
XLA Modules:
  0.0 51.4 jit_solution(6711474610523037350)
XLA Ops:
  0.6 48.1 %shard_map.158 = (f32[4,4,8]{2,1,0:T(4,128)}, f32[3,4,4,8]{3,2,1,0:T(4,128)}) custom-call(f32[3,4,4,8]{3,2,1,0:T(4,128)} %bitcast.7, s32[4,4,8]{2,1,0:T(4,128)} %bitcast.9, s32[4,4,8]{2,1,0:T(4,128)} %bitcast.10, s32[8,4,4,12]{3,2,1,0:T(4,128)} %refs_3_.1, bf16[10,128]{1,0:T(8,128)(2,1)} %refs_4_.1, bf16[2,8,64]{2,1,0:T(8,128)(2,1)} %refs_5_.1, ...), custom_call_target="tpu_custom_call" | custom-call | tf_op jit(solution)/shard_map/pallas_call | solution.py:571
  48.7 1.3 %copy.19 = f32[8,4,4]{0,2,1:T(4,128)} copy(f32[8,4,4]{0,2,1:T(4,128)} %bitcast.11) | data formatting | bytes 1024
  50.0 1.3 %copy.20 = f32[3,8,4,4]{1,3,2,0:T(4,128)} copy(f32[3,8,4,4]{1,3,2,0:T(4,128)} %bitcast.8) | data formatting | bytes 3072

commit v2 on v1

--- a/solution.py
+++ b/solution.py
@@ -83,17 +83,22 @@
 
     gx = lax.axis_index("gx")
     gy = lax.axis_index("gy")
+
+    def computed_at(x_block):
+        return jnp.where(x_block // 16 % 2 == 1, x_block // 16 * 16 + 12 - x_block // 4 % 4 * 4 + x_block % 4, x_block)
+
+    block = computed_at(gx)
     j, c = gy // 2, gy % 2
     own_half, own_slot = gy // 4, gy % 4
     edge = (gy == 3) | (gy == 4)
     halo_gy = 4 - c
     first, last_gx = gx == 0, gx == n_gx - 1
-    has_left = jnp.logical_not((j == 0) & first)
-    has_right = jnp.logical_not((j == 3) & last_gx)
+    has_left = jnp.logical_not((j == 0) & (block == 0))
+    has_right = jnp.logical_not((j == 3) & (block == n_gx - 1))
     has_other = ((j == 0) | (j == 3)) & has_left & has_right
-    other_gx = jnp.where(j == 0, gx - 1, gx + 1)
-    left = (jnp.where(j == 0, gx - 1, gx), jnp.where(j == 0, 6, 2 * j - 2))
-    right = (jnp.where(j == 3, gx + 1, gx), jnp.where(j == 3, 0, 2 * j + 2))
+    other_gx = jnp.where(j == 0, block - 1, block + 1)
+    left = (computed_at(jnp.where(j == 0, block - 1, block)), jnp.where(j == 0, 6, 2 * j - 2))
+    right = (computed_at(jnp.where(j == 3, block + 1, block)), jnp.where(j == 3, 0, 2 * j + 2))
     always = gx >= 0
     regions = (
         (has_left, (left[0], left[1] + c), 0, 128),
@@ -108,7 +113,8 @@
         for m in range(5):
             owner_gy = 4 * c + m if m < 4 else halo_gy
             if group == 0:
-                owners.append((owner_gy != gy, owner_gy == gy, (gx, owner_gy)))
+                here = (owner_gy == gy) & (block == gx)
+                owners.append((jnp.logical_not(here), here, (block, owner_gy)))
             else:
                 owners.append((has_other, None, (other_gx, owner_gy)))
     readers = []
@@ -117,10 +123,10 @@
         slot = own_slot if side == 0 else 4
         wanted = always if side == 0 else edge
         for p in range(4):
-            here = 2 * p + half == gy
-            readers.append((wanted & jnp.logical_not(here), wanted & here, (gx, 2 * p + half), slot))
-        readers.append((wanted & jnp.logical_not(first), None, (gx - 1, 6 + half), slot + 5))
-        readers.append((wanted & jnp.logical_not(last_gx), None, (gx + 1, half), slot + 5))
+            here = (2 * p + half == gy) & (block == gx)
+            readers.append((wanted & jnp.logical_not(here), wanted & here, (computed_at(gx), 2 * p + half), slot))
+        readers.append((wanted & jnp.logical_not(first), None, (computed_at(gx - 1), 6 + half), slot + 5))
+        readers.append((wanted & jnp.logical_not(last_gx), None, (computed_at(gx + 1), half), slot + 5))
 
     rcv1[...] = jnp.zeros_like(rcv1)
     rcv2[...] = jnp.zeros_like(rcv2)
@@ -192,7 +198,8 @@
     tile[8:24, :] = nb[...].T[0:16]
 
     pl.semaphore_wait(barrier, greetings)
-    for at, (there, here, device, slot) in enumerate(readers):
+    for at in (4, 5, 0, 1, 2, 3, 10, 11, 6, 7, 8, 9):
+        there, here, device, slot = readers[at]
         rows = 24 if at < 4 else 8
         send(there, here, device, tile.at[0:rows], rcv1.at[slot, 0:rows], 0, at, slot)
 
@@ -275,9 +282,12 @@
 
     present = geo[3:4, 0:SITES]
     own_hot = ext_hot[:, 0:SITES]
-    for layer in range(LAYERS):
+
+    def species_weights(layer):
         for k in range(4):
             mix[layer, k] = dot_exact(pw_ref[layer, :, k, :], own_hot[0:10], TN)
+
+    species_weights(0)
     h0 = dot(emb_ref[...].astype(F32), own_hot[0:10], TN) * present
 
     def rows_of(ref, m):
@@ -411,6 +421,7 @@
         source = snd2.at[0:128] if r < 2 else snd2.at[128:144]
         start = regions[facing[r]][2]
         send(there, None, device, source, rcv2.at[start : start + size], 1, r, facing[r])
+    species_weights(1)
     radial(1)
     near = dot(u1, oh[0:SITES, :])
     for r, (there, _, start, size) in enumerate(regions):
@@ -506,7 +517,8 @@
             tiles[1] = jnp.where(lane // 8 == jnp.where(other, at, -1), moved, tiles[1])
     snd4[4] = tiles[0]
     snd4[9] = tiles[1]
-    for at, (there, here, device) in enumerate(owners):
+    for at in (5, 6, 7, 8, 9, 0, 1, 2, 3, 4):
+        there, here, device = owners[at]
         slot = j if at < 5 else jnp.where(j == 0, 5, 4)
         slot = slot + (6 if at % 5 == 4 else 0)
         send(there, here, device, snd4.at[at], rcv4.at[slot], 3, at, slot)
@@ -609,9 +621,9 @@
             pltpu.SemaphoreType.DMA((4, 12)),
         ],
         compiler_params=pltpu.CompilerParams(
-            collective_id=0, has_side_effects=True, vmem_limit_bytes=60 * 1024 * 1024
+            collective_id=0, has_side_effects=True, vmem_limit_bytes=48 * 1024 * 1024
         ),
-    )(*operands)
+    )(*[pltpu.with_memory_space_constraint(one, pltpu.HBM) for one in operands])
     return energies.transpose(2, 0, 1), forces.transpose(0, 3, 1, 2)
 
 

time: 51.6 us -> 47.1 us (0.913)
  Pallas kernels: 48.1 us -> 45.1 us
  local copies, waits for them, and re-layouts: 2.64 us -> 1.21 us
    pallas_call x1, Pallas kernels: 48.1 us -> 45.1 us  [shards(): pl.pallas_call(functools.partial(kernel, n_gx), out_shape=(jax.ShapeDtype...]
    unnamed x2, local copies, waits for them, and re-layouts: 2.64 us -> 1.21 us
where the time goes in v2:
time: 47.1 us; the launch traced here: 46.9 us
  Pallas kernels  45.1 us (96%)
  local copies, waits for them, and re-layouts  1.21 us (3%)
  between operations  0.64 us (1%)
    pallas_call x1, Pallas kernels, shards(): pl.pallas_call(functools.partial(kernel, n_gx), out_shape=(jax.ShapeDtype...  45.1 us
    unnamed x2, local copies, waits for them, and re-layouts  1.21 us

profile of v2, /device:TPU:7, one launch (start us, length us, event | category | flops | bytes accessed | tf_op | source)
XLA Modules:
  0.0 46.9 jit_solution(13867544771428197599)
XLA Ops:
  0.6 45.1 %shard_map.158 = (f32[4,4,8]{2,1,0:T(4,128)S(1)}, f32[3,4,4,8]{3,2,1,0:T(4,128)S(1)}) custom-call(f32[3,4,4,8]{3,2,1,0:T(4,128)} %bitcast.9, s32[4,4,8]{2,1,0:T(4,128)} %bitcast.10, s32[4,4,8]{2,1,0:T(4,128)} %bitcast.11, s32[8,4,4,12]{3,2,1,0:T(4,128)} %refs_3_.1, bf16[10,128]{1,0:T(8,128)(2,1)} %refs_4_.1, bf16[2,8,64]{2,1,0:T(8,128)(2,1)} %refs_5_.1, ...), custom_call_target="tpu_custom_call" | custom-call | tf_op jit(solution)/shard_map/pallas_call | solution.py:583
  45.7 0.6 %copy.19 = f32[8,4,4]{0,2,1:T(4,128)} copy(f32[8,4,4]{0,2,1:T(4,128)S(1)} %bitcast.8) | data formatting | bytes 1024
  46.3 0.6 %copy.20 = f32[3,8,4,4]{1,3,2,0:T(4,128)} copy(f32[3,8,4,4]{1,3,2,0:T(4,128)S(1)} %bitcast.7) | data formatting | bytes 3072

commit v3 on v2

--- a/solution.py
+++ b/solution.py
@@ -63,6 +63,7 @@
 ROOT5 = math.sqrt(5.0)
 ROOT15 = math.sqrt(15.0)
 FACTOR = 1.0 / math.sqrt(SLOTS)
+GROUP = 4
 
 
 def kernel(n_gx, *refs):
@@ -71,6 +72,7 @@
     held, refs = refs[:15], refs[15:]
     (raw, nb, tile, geo, ps, oh, rcv1, snd2, rcv2, snd3, rcv3, snd4, rcv4), refs = refs[:13], refs[13:]
     (gs, bs, ye, bd, mix, dsilu, q, u, a, msg, dq, du, s_acc), refs = refs[:13], refs[13:]
+    (w1_t, w2_t, w3_t, w4_t, ow_t, up_t, fq, rows_held), refs = refs[:8], refs[8:]
     fetch_sem, send_sem, recv_sem = refs
     (pos_ref, occ_ref, spec_ref, nbr_ref, emb_ref, w1_ref, w2_ref, w3_ref, w4_ref), more = held[:9], held[9:]
     up_ref, pw_ref, ow_ref, rl_ref, rh_ref, rlast_ref = more
@@ -180,7 +182,8 @@
     raw[...] = jnp.zeros_like(raw)
     nb[...] = jnp.zeros_like(nb)
     tile[...] = jnp.zeros_like(tile)
-    x_pick = (iota((SITES, SITES), 0) == iota((SITES, SITES), 1) // 16).astype(F32)
+    x_pick = (iota((SITES, SITES), 0) == iota((SITES, SITES), 1) // 16)
+    x_pick = jnp.where(x_pick, 1.0, 0.0).astype(BF16)
     yz_mask = iota((80, SITES), 0) % 16 == iota((80, SITES), 1) % 16
     for i in range(4):
         fetches[i].wait()
@@ -192,7 +195,8 @@
     for x in range(8):
         for y in range(4):
             nb[x * 16 + y * 4 : x * 16 + y * 4 + 4, 0:SLOTS] = nbr_ref[x, y].astype(F32)
-    spread = jnp.where(yz_mask, dot_exact(raw[...], x_pick), 0.0)
+    spread = dot(split3(raw[...]), x_pick)
+    spread = jnp.where(yz_mask, spread[0:80] + spread[80:160] + spread[160:240], 0.0)
     for f in range(5):
         tile[f : f + 1, :] = jnp.sum(spread[f * 16 : f * 16 + 16], axis=0, keepdims=True)
     tile[8:24, :] = nb[...].T[0:16]
@@ -210,13 +214,16 @@
     ps[...] = jnp.where(hit, 1.0, 0.0).astype(BF16)
     for i in range(4, 15):
         fetches[i].wait()
+    for layer in range(LAYERS):
+        for ref, turned in ((w1_ref, w1_t), (w2_ref, w2_t), (w3_ref, w3_t), (w4_ref, w4_t), (ow_ref, ow_t)):
+            turned[layer] = ref[layer].T
+    up_t[...] = up_ref[1].T
     lifted_table = dot(emb_ref[...], up_ref[0]).astype(BF16).astype(F32)
     s_acc[...] = jnp.zeros_like(s_acc)
     geo[...] = jnp.zeros_like(geo)
 
-    for slot in range(10):
-        rows = 24 if slot < 4 else 8
-        receive(always if slot < 5 else has_other, rcv1.at[slot, 0:rows], 0, slot)
+    for slot in range(4):
+        receive(always, rcv1.at[slot, 0:24], 0, slot)
 
     lane = iota((8, SITES), 1)
     no = gx < 0
@@ -233,7 +240,8 @@
     def strip_shift(x0, r, x):
         return lax.rem(2 * SITES + r * 16 + x * 8 - (x0 + x) * 16 - y_halo * 4, SITES)
 
-    for r, (x0, other) in enumerate(slabs):
+    def slab(r):
+        x0, other = slabs[r]
         out = jnp.zeros((8, SITES), F32)
         for m in range(4):
             source = rcv1[m, 0:8]
@@ -243,15 +251,8 @@
                 moved = pltpu.roll(source, slab_shift(x0, m, x), 1)
                 out = jnp.where(lane // 16 == x * 4 + m, moved, out)
         geo[:, r * SITES : (r + 1) * SITES] = out
-    out = jnp.zeros((8, SITES), F32)
-    for r, (x0, other) in enumerate(slabs):
-        source = rcv1[4, 0:8]
-        if r > 0:
-            source = jnp.where(other, rcv1[9, 0:8], source)
-        for x in range(2):
-            moved = pltpu.roll(source, strip_shift(x0, r, x), 1)
-            out = jnp.where(lane // 8 == r * 2 + x, moved, out)
-    geo[:, 3 * SITES : 4 * SITES] = out
+
+    slab(0)
 
     lane16 = iota((16, SITES), 1)
     index = jnp.zeros((16, SITES), F32)
@@ -272,23 +273,37 @@
         hit = ext_row == place[k : k + 1]
         oh[:, k * SITES : (k + 1) * SITES] = jnp.where(hit, 1.0, 0.0).astype(BF16)
 
+    present = geo[3:4, 0:SITES]
+    own_hot = (geo[4:5, 0:SITES].astype(jnp.int32) == iota((16, SITES), 0)).astype(F32)
+
+    def species_weights(layer):
+        for k in range(4):
+            mix[layer, k] = dot_exact(pw_ref[layer, :, k, :], own_hot[0:10], TN)
+
+    species_weights(0)
+    h0 = dot(emb_ref[...].astype(F32), own_hot[0:10], TN) * present
+
+    for slot in range(4, 10):
+        receive(always if slot < 5 else has_other, rcv1.at[slot, 0:8], 0, slot)
+    slab(1)
+    slab(2)
+    out = jnp.zeros((8, SITES), F32)
+    for r, (x0, other) in enumerate(slabs):
+        source = rcv1[4, 0:8]
+        if r > 0:
+            source = jnp.where(other, rcv1[9, 0:8], source)
+        for x in range(2):
+            moved = pltpu.roll(source, strip_shift(x0, r, x), 1)
+            out = jnp.where(lane // 8 == r * 2 + x, moved, out)
+    geo[:, 3 * SITES : 4 * SITES] = out
+
     gathered = dot(split3(geo[:, 0:EXT]), oh[...])
     gathered = gathered[0:8] + gathered[8:16] + gathered[16:24]
     for k in range(SLOTS):
         gs[k * 8 : k * 8 + 8, :] = gathered[:, k * SITES : (k + 1) * SITES]
     ext_hot = (geo[4:5, 0:EXT].astype(jnp.int32) == iota((16, EXT), 0)).astype(F32)
     u0 = dot(lifted_table, ext_hot[0:10], TN).astype(BF16)
-    u[0] = dot(u0, oh[...])
-
-    present = geo[3:4, 0:SITES]
-    own_hot = ext_hot[:, 0:SITES]
-
-    def species_weights(layer):
-        for k in range(4):
-            mix[layer, k] = dot_exact(pw_ref[layer, :, k, :], own_hot[0:10], TN)
-
-    species_weights(0)
-    h0 = dot(emb_ref[...].astype(F32), own_hot[0:10], TN) * present
+    u[0] = dot(u0, oh[...]).astype(BF16)
 
     def rows_of(ref, m):
         return ref[pl.ds(m, SLOTS, stride=8), :]
@@ -320,9 +335,10 @@
         ROOT15 * nx * nz,
         0.5 * ROOT15 * (nx * nx - ny * ny),
     ]
-    ye[0, 0:SLOTS] = ye_scale
-    for m in range(8):
-        ye[m + 1, 0:SLOTS] = ye_scale * harmonics[m]
+    for m in range(9):
+        one = ye_scale if m == 0 else ye_scale * harmonics[m - 1]
+        for k in range(SLOTS):
+            ye[m, k] = jnp.broadcast_to(one[k : k + 1], (16, SITES)).astype(BF16)
     theta = math.pi * scaled
     sin1 = jnp.sin(theta)
     cos1 = jnp.cos(theta)
@@ -340,24 +356,32 @@
     def radial(layer):
         hidden = jnp.concatenate([bs[k * 8 : k * 8 + 8, :] for k in range(SLOTS)], axis=1)
         hidden = hidden.astype(BF16)
-        for step, ref in enumerate((w1_ref, w2_ref, w3_ref)):
-            z = dot(ref[layer], hidden, TN)
+        for step, ref in enumerate((w1_t, w2_t, w3_t)):
+            z = dot(ref[layer], hidden)
             g, slope_g = silu_parts(z)
             dsilu[layer, step] = slope_g
             hidden = g.astype(BF16)
-        q[layer] = dot(w4_ref[layer], hidden, TN)
+        q[layer] = dot(w4_t[layer], hidden).astype(BF16)
+
+    def harmonic(m, k):
+        return jnp.concatenate([ye[m, k], ye[m, k]], axis=0)
 
     def aggregate(layer):
         def body(block, carry):
             c0 = pl.multiple_of(block * 32, 32)
-            acc = [jnp.zeros((32, SITES), F32) for _ in range(9)]
-            for k in range(SLOTS):
-                lanes = slice(k * SITES, (k + 1) * SITES)
-                uk = u[layer, pl.ds(c0, 32), lanes]
-                v = [q[layer, pl.ds(L * CH + c0, 32), lanes] * uk for L in range(3)]
+            acc = [None] * 9
+            for first_k in range(0, SLOTS, GROUP):
+                some = [None] * 9
+                for k in range(first_k, first_k + GROUP):
+                    lanes = slice(k * SITES, (k + 1) * SITES)
+                    uk = u[layer, pl.ds(c0, 32), lanes]
+                    v = [q[layer, pl.ds(L * CH + c0, 32), lanes] * uk for L in range(3)]
+                    for m in range(9):
+                        term = harmonic(m, k) * v[0 if m == 0 else (1 if m < 4 else 2)]
+                        some[m] = term if some[m] is None else some[m] + term
                 for m in range(9):
-                    degree = 0 if m == 0 else (1 if m < 4 else 2)
-                    acc[m] = acc[m] + ye[m, k : k + 1, :] * v[degree]
+                    one = some[m].astype(F32)
+                    acc[m] = one if acc[m] is None else acc[m] + one
             for m in range(9):
                 a[layer, m, pl.ds(c0, 32), :] = acc[m]
             p = [mix[layer, j, pl.ds(c0, 32), :] for j in range(4)]
@@ -370,39 +394,75 @@
 
         lax.fori_loop(0, CH // 32, body, 0)
 
-    def aggregate_back(layer, msg_grad_ref, with_du):
-        def body(block, carry):
-            c0 = pl.multiple_of(block * 32, 32)
-            g = msg_grad_ref[pl.ds(c0, 32), :]
-            p = [mix[layer, j, pl.ds(c0, 32), :] for j in range(4)]
-            a0 = a[layer, 0, pl.ds(c0, 32), :]
-            scale1 = 2.0 * p[2] * g
-            scale2 = 2.0 * p[3] * g
-            da = [g * (p[0] + 2.0 * p[1] * a0)]
-            for m in range(1, 9):
-                da.append((scale1 if m < 4 else scale2) * a[layer, m, pl.ds(c0, 32), :])
-            for k in range(SLOTS):
-                lanes = slice(k * SITES, (k + 1) * SITES)
-                uk = u[layer, pl.ds(c0, 32), lanes]
-                qk = [q[layer, pl.ds(L * CH + c0, 32), lanes] for L in range(3)]
-                v = [one * uk for one in qk]
-                dv = [None, None, None]
-                for m in range(9):
-                    degree = 0 if m == 0 else (1 if m < 4 else 2)
-                    term = ye[m, k : k + 1, :] * da[m]
-                    dv[degree] = term if dv[degree] is None else dv[degree] + term
-                    part = da[m] * v[degree]
-                    part = part[0:8] + part[8:16] + part[16:24] + part[24:32]
-                    at = (m * SLOTS + k) * 8
-                    s_acc[at : at + 8, :] += part
+    def slopes(layer, c0):
+        p = [mix[layer, j, pl.ds(c0, 32), :] for j in range(1, 4)]
+        out = [mix[layer, 0, pl.ds(c0, 32), :] + 2.0 * p[0] * a[layer, 0, pl.ds(c0, 32), :]]
+        for m in range(1, 9):
+            out.append((2.0 * p[1 if m < 4 else 2]) * a[layer, m, pl.ds(c0, 32), :])
+        return out
+
+    def by_degree(da, k):
+        out = [harmonic(0, k) * da[0], None, None]
+        for m in range(1, 9):
+            degree = 1 if m < 4 else 2
+            term = harmonic(m, k) * da[m]
+            out[degree] = term if out[degree] is None else out[degree] + term
+        return out
+
+    def blocks(body):
+        def step(block, carry):
+            body(pl.multiple_of(block * 32, 32))
+            return carry
+
+        lax.fori_loop(0, CH // 32, step, 0)
+
+    def prepare_first(c0):
+        t = slopes(0, c0)
+        for m in range(9):
+            a[0, m, pl.ds(c0, 32), :] = t[m]
+        t = [one.astype(BF16) for one in t]
+        for k in range(SLOTS):
+            lanes = slice(k * SITES, (k + 1) * SITES)
+            uk = u[0, pl.ds(c0, 32), lanes]
+            for L, one in enumerate(by_degree(t, k)):
+                fq[pl.ds(L * CH + c0, 32), lanes] = one * uk
+
+    def features_back(c0):
+        g = bm[pl.ds(c0, 32), :]
+        da = [g * one for one in slopes(1, c0)]
+        for m in range(9):
+            a[1, m, pl.ds(c0, 32), :] = da[m]
+        da = [one.astype(BF16) for one in da]
+        for k in range(SLOTS):
+            lanes = slice(k * SITES, (k + 1) * SITES)
+            uk = u[1, pl.ds(c0, 32), lanes]
+            dv = by_degree(da, k)
+            total = dv[0] * q[1, pl.ds(c0, 32), lanes]
+            for L in range(1, 3):
+                total = total + dv[L] * q[1, pl.ds(L * CH + c0, 32), lanes]
+            du[pl.ds(c0, 32), lanes] = total
+            for L in range(3):
+                dq[pl.ds(L * CH + c0, 32), lanes] = dv[L] * uk
+
+    def angular_back(layer, c0):
+        da = [a[layer, m, pl.ds(c0, 32), :] for m in range(9)]
+        if layer == 0:
+            g = bm[pl.ds(c0, 32), :]
+            da = [g * one for one in da]
+            g = g.astype(BF16)
+        da = [one.astype(BF16) for one in da]
+        for k in range(SLOTS):
+            lanes = slice(k * SITES, (k + 1) * SITES)
+            uk = u[layer, pl.ds(c0, 32), lanes]
+            v = [q[layer, pl.ds(L * CH + c0, 32), lanes] * uk for L in range(3)]
+            for m in range(9):
+                part = da[m] * v[0 if m == 0 else (1 if m < 4 else 2)]
+                at = (m * SLOTS + k) * 8
+                part = (part[0:16] + part[16:32]).astype(F32)
+                s_acc[at : at + 8, :] += part[0:8] + part[8:16]
+            if layer == 0:
                 for L in range(3):
-                    dq[pl.ds(L * CH + c0, 32), lanes] = (dv[L] * uk).astype(BF16)
-                if with_du:
-                    total = dv[0] * qk[0] + dv[1] * qk[1] + dv[2] * qk[2]
-                    du[pl.ds(c0, 32), lanes] = total.astype(BF16)
-            return carry
-
-        lax.fori_loop(0, CH // 32, body, 0)
+                    dq[pl.ds(L * CH + c0, 32), lanes] = g * fq[pl.ds(L * CH + c0, 32), lanes]
 
     def radial_back(layer):
         grad = dot(w4_ref[layer], dq[...])
@@ -411,24 +471,31 @@
             grad = dot(ref[layer], dz)
         return grad
 
+    bm = nb
     radial(0)
     aggregate(0)
-    mixed = dot(ow_ref[0], msg[...], TN)
+    mixed = dot(ow_t[0], msg[...])
     h1 = (h0 + present * mixed).astype(BF16)
-    u1 = dot(up_ref[1], h1, TN).astype(BF16)
-    snd2[...] = dot(ps[128:272, :], u1, NT).astype(BF16)
+    u1_rows = dot(h1, up_ref[1], TN)
+    rows_held[...] = u1_rows
+    snd2[0:128] = u1_rows.astype(BF16)
+    y_rows = pl.multiple_of(y_strip * 4, 8)
+    strip = [rows_held[pl.ds(y_rows + x * 64, 8), :] for x in range(2)]
+    snd2[128:144] = jnp.concatenate(strip, axis=0).astype(BF16)
+    u1 = dot(up_t[...], h1).astype(BF16)
     for r, (there, device, start, size) in enumerate(regions):
         source = snd2.at[0:128] if r < 2 else snd2.at[128:144]
         start = regions[facing[r]][2]
         send(there, None, device, source, rcv2.at[start : start + size], 1, r, facing[r])
     species_weights(1)
+    blocks(prepare_first)
     radial(1)
     near = dot(u1, oh[0:SITES, :])
     for r, (there, _, start, size) in enumerate(regions):
         receive(there, rcv2.at[start : start + size], 1, r)
-    u[1] = near + dot(rcv2[...], oh[SITES:EXT, :], TN)
+    u[1] = (near + dot(rcv2[...], oh[SITES:EXT, :], TN)).astype(BF16)
     aggregate(1)
-    mixed = dot(ow_ref[1], msg[...], TN)
+    mixed = dot(ow_t[1], msg[...])
     h2 = (h1.astype(F32) + present * mixed).astype(BF16)
 
     diagonal = iota((CH, CH), 0) == iota((CH, CH), 1)
@@ -443,9 +510,8 @@
     dh2 = dot(rh_ref[...], dz, TN)
     dmixed = (present * dh2).astype(BF16)
     message_grad = dot(ow_ref[1], dmixed)
-    bm = nb
     bm[...] = message_grad
-    aggregate_back(1, bm, True)
+    blocks(features_back)
     snd3[...] = dot(oh[SITES:EXT, :], du[...], NT).astype(BF16)
     for r, (there, device, start, size) in enumerate(regions):
         target = regions[facing[r]][2]
@@ -453,13 +519,14 @@
         send(there, None, device, source, rcv3.at[target : target + size], 2, r, facing[r])
     near = dot(du[...], oh[0:SITES, :], NT)
     bessel_grad = radial_back(1)
+    blocks(functools.partial(angular_back, 1))
     for r, (there, _, start, size) in enumerate(regions):
         receive(there, rcv3.at[start : start + size], 2, r)
     du1 = near + dot(rcv3[...], ps[...], TN)
     dh1 = dh2 + linear * present + dot(up_ref[1], du1.astype(BF16))
     dmixed = (present * dh1).astype(BF16)
     bm[...] = dot(ow_ref[0], dmixed)
-    aggregate_back(0, bm, False)
+    blocks(functools.partial(angular_back, 0))
     bessel_grad = bessel_grad + radial_back(0)
 
     for k in range(SLOTS):
@@ -522,6 +589,15 @@
         slot = j if at < 5 else jnp.where(j == 0, 5, 4)
         slot = slot + (6 if at % 5 == 4 else 0)
         send(there, here, device, snd4.at[at], rcv4.at[slot], 3, at, slot)
+
+    def settle(some):
+        for there, remote in some:
+
+            @pl.when(there)
+            def _():
+                remote().wait_send()
+
+    settle(sent[:-10])
     for at, (there, here, _, _) in enumerate(readers):
         wanted = there if here is None else there | here
         receive(wanted, rcv4.at[at], 3, at)
@@ -532,16 +608,13 @@
     rows = [jnp.broadcast_to(-back[axis : axis + 1], (16, SITES)) for axis in range(3)]
     rows.append(jnp.broadcast_to(back[3:4], (16, SITES)))
     full = jnp.where(yz_mask[0:64], jnp.concatenate(rows, axis=0), 0.0)
-    out = dot_exact(full, x_pick, NT)
+    out = dot(split3(full), x_pick, NT)
+    out = out[0:64] + out[64:128] + out[128:192]
     for y in range(4):
         for axis in range(3):
             force_ref[axis, y] = out[axis * 16 + y * 4 : axis * 16 + y * 4 + 4, 0:8]
         en_ref[y] = out[48 + y * 4 : 52 + y * 4, 0:8]
-    for there, remote in sent:
-
-        @pl.when(there)
-        def _():
-            remote().wait_send()
+    settle(sent[-10:])
 
 
 def shards(
@@ -605,17 +678,25 @@
             pltpu.VMEM((12, 8, SITES), F32),
             pltpu.VMEM((SLOTS * 8, SITES), F32),
             pltpu.VMEM((SLOTS * 8, SITES), F32),
-            pltpu.VMEM((9, 16, SITES), F32),
+            pltpu.VMEM((9, SLOTS, 16, SITES), BF16),
             pltpu.VMEM((BES, 16, SITES), F32),
             pltpu.VMEM((LAYERS, 4, CH, SITES), F32),
             pltpu.VMEM((LAYERS, 3, RAD, EDGES), F32),
-            pltpu.VMEM((LAYERS, 3 * CH, EDGES), F32),
-            pltpu.VMEM((LAYERS, CH, EDGES), F32),
+            pltpu.VMEM((LAYERS, 3 * CH, EDGES), BF16),
+            pltpu.VMEM((LAYERS, CH, EDGES), BF16),
             pltpu.VMEM((LAYERS, 9, CH, SITES), F32),
             pltpu.VMEM((CH, SITES), BF16),
             pltpu.VMEM((3 * CH, EDGES), BF16),
             pltpu.VMEM((CH, EDGES), BF16),
             pltpu.VMEM((9 * SLOTS * 8, SITES), F32),
+            pltpu.VMEM((LAYERS, RAD, BES), BF16),
+            pltpu.VMEM((LAYERS, RAD, RAD), BF16),
+            pltpu.VMEM((LAYERS, RAD, RAD), BF16),
+            pltpu.VMEM((LAYERS, 3 * CH, RAD), BF16),
+            pltpu.VMEM((LAYERS, CH, CH), BF16),
+            pltpu.VMEM((CH, CH), BF16),
+            pltpu.VMEM((3 * CH, EDGES), BF16),
+            pltpu.VMEM((SITES, CH), F32),
             pltpu.SemaphoreType.DMA((15,)),
             pltpu.SemaphoreType.DMA((4, 12)),
             pltpu.SemaphoreType.DMA((4, 12)),

time: 47.1 us -> 44.5 us (0.945)
  Pallas kernels: 45.1 us -> 42.5 us
    pallas_call x1, Pallas kernels: 45.1 us -> 42.5 us  [shards(): pl.pallas_call(functools.partial(kernel, n_gx), out_shape=(jax.ShapeDtype...]
where the time goes in v3:
time: 44.5 us; the launch traced here: 44.4 us
  Pallas kernels  42.5 us (96%)
  local copies, waits for them, and re-layouts  1.21 us (3%)
  between operations  0.64 us (1%)
    pallas_call x1, Pallas kernels, shards(): pl.pallas_call(functools.partial(kernel, n_gx), out_shape=(jax.ShapeDtype...  42.5 us
    unnamed x2, local copies, waits for them, and re-layouts  1.21 us

profile of v3, /device:TPU:7, one launch (start us, length us, event | category | flops | bytes accessed | tf_op | source)
XLA Modules:
  0.0 44.4 jit_solution(5849090293518856255)
XLA Ops:
  0.6 42.5 %shard_map.158 = (f32[4,4,8]{2,1,0:T(4,128)S(1)}, f32[3,4,4,8]{3,2,1,0:T(4,128)S(1)}) custom-call(f32[3,4,4,8]{3,2,1,0:T(4,128)} %bitcast.9, s32[4,4,8]{2,1,0:T(4,128)} %bitcast.10, s32[4,4,8]{2,1,0:T(4,128)} %bitcast.11, s32[8,4,4,12]{3,2,1,0:T(4,128)} %refs_3_.1, bf16[10,128]{1,0:T(8,128)(2,1)} %refs_4_.1, bf16[2,8,64]{2,1,0:T(8,128)(2,1)} %refs_5_.1, ...), custom_call_target="tpu_custom_call" | custom-call | tf_op jit(solution)/shard_map/pallas_call | solution.py:656
  43.2 0.6 %copy.19 = f32[8,4,4]{0,2,1:T(4,128)} copy(f32[8,4,4]{0,2,1:T(4,128)S(1)} %bitcast.8) | data formatting | bytes 1024
  43.8 0.6 %copy.20 = f32[3,8,4,4]{1,3,2,0:T(4,128)} copy(f32[3,8,4,4]{1,3,2,0:T(4,128)S(1)} %bitcast.7) | data formatting | bytes 3072

commit v4 on v3

--- a/solution.py
+++ b/solution.py
@@ -76,12 +76,6 @@
     fetch_sem, send_sem, recv_sem = refs
     (pos_ref, occ_ref, spec_ref, nbr_ref, emb_ref, w1_ref, w2_ref, w3_ref, w4_ref), more = held[:9], held[9:]
     up_ref, pw_ref, ow_ref, rl_ref, rh_ref, rlast_ref = more
-
-    fetches = []
-    for i in range(15):
-        fetch = pltpu.make_async_copy(inputs[i], held[i], fetch_sem.at[i])
-        fetch.start()
-        fetches.append(fetch)
 
     gx = lax.axis_index("gx")
     gy = lax.axis_index("gy")
@@ -141,10 +135,17 @@
         def _():
             pl.semaphore_signal(barrier, inc=1, device_id=device, device_id_type=MESH)
 
-    for there, _, device in owners:
+    for there, _, device in owners[5:]:
         greet(there, device)
-    for there, device, _, _ in regions:
+    for there, device, _, _ in regions[:2] + regions[3:] + regions[2:3]:
         greet(there, device)
+    for there, _, device in owners[:5]:
+        greet(there, device)
+    fetches = []
+    for i in range(15):
+        fetch = pltpu.make_async_copy(inputs[i], held[i], fetch_sem.at[i])
+        fetch.start()
+        fetches.append(fetch)
     greetings = jnp.int32(0)
     for there, _, _, _ in readers + list(regions):
         greetings = greetings + there.astype(jnp.int32)
@@ -185,27 +186,35 @@
     x_pick = (iota((SITES, SITES), 0) == iota((SITES, SITES), 1) // 16)
     x_pick = jnp.where(x_pick, 1.0, 0.0).astype(BF16)
     yz_mask = iota((80, SITES), 0) % 16 == iota((80, SITES), 1) % 16
-    for i in range(4):
+    for i in range(3):
         fetches[i].wait()
     for y in range(4):
         for axis in range(3):
             raw[axis * 16 + y * 4 : axis * 16 + y * 4 + 4, 0:8] = pos_ref[axis, y]
         raw[48 + y * 4 : 52 + y * 4, 0:8] = occ_ref[y].astype(F32)
         raw[64 + y * 4 : 68 + y * 4, 0:8] = spec_ref[y].astype(F32)
-    for x in range(8):
-        for y in range(4):
-            nb[x * 16 + y * 4 : x * 16 + y * 4 + 4, 0:SLOTS] = nbr_ref[x, y].astype(F32)
     spread = dot(split3(raw[...]), x_pick)
     spread = jnp.where(yz_mask, spread[0:80] + spread[80:160] + spread[160:240], 0.0)
     for f in range(5):
         tile[f : f + 1, :] = jnp.sum(spread[f * 16 : f * 16 + 16], axis=0, keepdims=True)
+
+    pl.semaphore_wait(barrier, greetings)
+
+    def send_tile(at, rows):
+        there, here, device, slot = readers[at]
+        send(there, here, device, tile.at[0:rows], rcv1.at[slot, 0:rows], 0, at, slot)
+
+    for at in (4, 5, 10, 11):
+        send_tile(at, 8)
+    fetches[3].wait()
+    for x in range(8):
+        for y in range(4):
+            nb[x * 16 + y * 4 : x * 16 + y * 4 + 4, 0:SLOTS] = nbr_ref[x, y].astype(F32)
     tile[8:24, :] = nb[...].T[0:16]
-
-    pl.semaphore_wait(barrier, greetings)
-    for at in (4, 5, 0, 1, 2, 3, 10, 11, 6, 7, 8, 9):
-        there, here, device, slot = readers[at]
-        rows = 24 if at < 4 else 8
-        send(there, here, device, tile.at[0:rows], rcv1.at[slot, 0:rows], 0, at, slot)
+    for at in range(4):
+        send_tile(at, 24)
+    for at in range(6, 10):
+        send_tile(at, 8)
 
     rows = iota((GHOSTS, SITES), 0)
     y_strip = 14 * (1 - c)
@@ -565,30 +574,28 @@
         geo[axis : axis + 1, 0:SITES] = geo[axis : axis + 1, 0:SITES] - centre[axis]
     geo[3:4, 0:SITES] = energy
 
-    for m in range(4):
-        tiles = [jnp.zeros((8, SITES), F32) for _ in range(2)]
-        for r, (x0, other) in enumerate(slabs):
-            for x in range(2):
-                moved = pltpu.roll(geo[:, r * SITES : (r + 1) * SITES], lax.rem(SITES - slab_shift(x0, m, x), SITES), 1)
-                tiles[0] = jnp.where(lane // 16 == jnp.where(other, -1, x0 + x), moved, tiles[0])
-                if r > 0:
-                    tiles[1] = jnp.where(lane // 16 == jnp.where(other, x0 + x, -1), moved, tiles[1])
-        snd4[m] = tiles[0]
-        snd4[5 + m] = tiles[1]
-    tiles = [jnp.zeros((8, SITES), F32) for _ in range(2)]
-    for r, (x0, other) in enumerate(slabs):
-        for x in range(2):
-            moved = pltpu.roll(geo[:, 3 * SITES :], lax.rem(SITES - strip_shift(x0, r, x), SITES), 1)
-            at = 2 * (x0 + x) + c
-            tiles[0] = jnp.where(lane // 8 == jnp.where(other, -1, at), moved, tiles[0])
-            tiles[1] = jnp.where(lane // 8 == jnp.where(other, at, -1), moved, tiles[1])
-    snd4[4] = tiles[0]
-    snd4[9] = tiles[1]
-    for at in (5, 6, 7, 8, 9, 0, 1, 2, 3, 4):
-        there, here, device = owners[at]
-        slot = j if at < 5 else jnp.where(j == 0, 5, 4)
-        slot = slot + (6 if at % 5 == 4 else 0)
-        send(there, here, device, snd4.at[at], rcv4.at[slot], 3, at, slot)
+    for group in (1, 0):
+        for m in range(5):
+            out = jnp.zeros((8, SITES), F32)
+            for r, (x0, other) in enumerate(slabs):
+                if group == 1 and r == 0:
+                    continue
+                for x in range(2):
+                    if m < 4:
+                        part, shift = r, slab_shift(x0, m, x)
+                        at, width = x0 + x, 16
+                    else:
+                        part, shift = 3, strip_shift(x0, r, x)
+                        at, width = 2 * (x0 + x) + c, 8
+                    moved = pltpu.roll(geo[:, part * SITES : (part + 1) * SITES], lax.rem(SITES - shift, SITES), 1)
+                    at = jnp.where(other, at, -1) if group == 1 else jnp.where(other, -1, at)
+                    out = jnp.where(lane // width == at, moved, out)
+            snd4[5 * group + m] = out
+        for at in range(5 * group, 5 * group + 5):
+            there, here, device = owners[at]
+            slot = j if group == 0 else jnp.where(j == 0, 5, 4)
+            slot = slot + (6 if at % 5 == 4 else 0)
+            send(there, here, device, snd4.at[at], rcv4.at[slot], 3, at, slot)
 
     def settle(some):
         for there, remote in some:

time: 44.5 us -> 43.9 us (0.987)
  Pallas kernels: 42.5 us -> 41.9 us
    pallas_call x1, Pallas kernels: 42.5 us -> 41.9 us  [shards(): pl.pallas_call(functools.partial(kernel, n_gx), out_shape=(jax.ShapeDtype...]
where the time goes in v4:
time: 43.9 us; the launch traced here: 43.8 us
  Pallas kernels  41.9 us (95%)
  local copies, waits for them, and re-layouts  1.21 us (3%)
  between operations  0.64 us (1%)
    pallas_call x1, Pallas kernels, shards(): pl.pallas_call(functools.partial(kernel, n_gx), out_shape=(jax.ShapeDtype...  41.9 us
    unnamed x2, local copies, waits for them, and re-layouts  1.21 us

profile of v4, /device:TPU:7, one launch (start us, length us, event | category | flops | bytes accessed | tf_op | source)
XLA Modules:
  0.0 43.8 jit_solution(1122167932899205962)
XLA Ops:
  0.6 41.9 %shard_map.158 = (f32[4,4,8]{2,1,0:T(4,128)S(1)}, f32[3,4,4,8]{3,2,1,0:T(4,128)S(1)}) custom-call(f32[3,4,4,8]{3,2,1,0:T(4,128)} %bitcast.9, s32[4,4,8]{2,1,0:T(4,128)} %bitcast.10, s32[4,4,8]{2,1,0:T(4,128)} %bitcast.11, s32[8,4,4,12]{3,2,1,0:T(4,128)} %refs_3_.1, bf16[10,128]{1,0:T(8,128)(2,1)} %refs_4_.1, bf16[2,8,64]{2,1,0:T(8,128)(2,1)} %refs_5_.1, ...), custom_call_target="tpu_custom_call" | custom-call | tf_op jit(solution)/shard_map/pallas_call | solution.py:663
  42.6 0.6 %copy.19 = f32[8,4,4]{0,2,1:T(4,128)} copy(f32[8,4,4]{0,2,1:T(4,128)S(1)} %bitcast.8) | data formatting | bytes 1024
  43.2 0.6 %copy.20 = f32[3,8,4,4]{1,3,2,0:T(4,128)} copy(f32[3,8,4,4]{1,3,2,0:T(4,128)S(1)} %bitcast.7) | data formatting | bytes 3072

commit v5 on v4

--- a/solution.py
+++ b/solution.py
@@ -68,7 +68,7 @@
 
 def kernel(n_gx, *refs):
     inputs, refs = refs[:15], refs[15:]
-    (en_ref, force_ref), refs = refs[:2], refs[2:]
+    out_ref, refs = refs[0], refs[1:]
     held, refs = refs[:15], refs[15:]
     (raw, nb, tile, geo, ps, oh, rcv1, snd2, rcv2, snd3, rcv3, snd4, rcv4), refs = refs[:13], refs[13:]
     (gs, bs, ye, bd, mix, dsilu, q, u, a, msg, dq, du, s_acc), refs = refs[:13], refs[13:]
@@ -619,8 +619,8 @@
     out = out[0:64] + out[64:128] + out[128:192]
     for y in range(4):
         for axis in range(3):
-            force_ref[axis, y] = out[axis * 16 + y * 4 : axis * 16 + y * 4 + 4, 0:8]
-        en_ref[y] = out[48 + y * 4 : 52 + y * 4, 0:8]
+            out_ref[axis, y] = out[axis * 16 + y * 4 : axis * 16 + y * 4 + 4, 0:8]
+        out_ref[3, y] = out[48 + y * 4 : 52 + y * 4, 0:8]
     settle(sent[-10:])
 
 
@@ -660,14 +660,11 @@
         read_hidden.T,
         read_last.reshape(1, -1),
     )
-    energies, forces = pl.pallas_call(
+    out = pl.pallas_call(
         functools.partial(kernel, n_gx),
-        out_shape=(
-            jax.ShapeDtypeStruct((4, 4, 8), F32),
-            jax.ShapeDtypeStruct((3, 4, 4, 8), F32),
-        ),
+        out_shape=jax.ShapeDtypeStruct((4, 4, 4, 8), F32),
         in_specs=[pl.BlockSpec(memory_space=pltpu.HBM)] * 15,
-        out_specs=(vmem, vmem),
+        out_specs=vmem,
         scratch_shapes=[pltpu.VMEM(one.shape, one.dtype) for one in operands]
         + [
             pltpu.VMEM((80, SITES), F32),
@@ -712,7 +709,7 @@
             collective_id=0, has_side_effects=True, vmem_limit_bytes=48 * 1024 * 1024
         ),
     )(*[pltpu.with_memory_space_constraint(one, pltpu.HBM) for one in operands])
-    return energies.transpose(2, 0, 1), forces.transpose(0, 3, 1, 2)
+    return out[3].transpose(2, 0, 1), out[:3].transpose(0, 3, 1, 2)
 
 
 def solution(mesh):

time: 43.9 us -> 43.9 us (level)
    transpose x0 -> x2, local copies, waits for them, and re-layouts: none -> 1.21 us  [shards(): return (out[3].transpose(2, 0, 1), out[:3].transpose(0, 3, 1, 2))]
    unnamed x2 -> x0, local copies, waits for them, and re-layouts: 1.21 us -> none
where the time goes in v5:
time: 43.9 us; the launch traced here: 43.8 us
  Pallas kernels  41.9 us (95%)
  local copies, waits for them, and re-layouts  1.21 us (3%)
  between operations  0.64 us (1%)
    pallas_call x1, Pallas kernels, shards(): pl.pallas_call(functools.partial(kernel, n_gx), out_shape=jax.ShapeDtypeS...  41.9 us
    transpose x2, local copies, waits for them, and re-layouts, shards(): return (out[3].transpose(2, 0, 1), out[:3].transpose(0, 3, 1, 2))  1.21 us

profile of v5, /device:TPU:7, one launch (start us, length us, event | category | flops | bytes accessed | tf_op | source)
XLA Modules:
  0.0 43.8 jit_solution(12286700840865646929)
XLA Ops:
  0.6 41.9 %shard_map.158 = f32[4,4,4,8]{3,2,1,0:T(4,128)S(1)} custom-call(f32[3,4,4,8]{3,2,1,0:T(4,128)} %bitcast.11, s32[4,4,8]{2,1,0:T(4,128)} %bitcast.12, s32[4,4,8]{2,1,0:T(4,128)} %bitcast.13, s32[8,4,4,12]{3,2,1,0:T(4,128)} %refs_3_.1, bf16[10,128]{1,0:T(8,128)(2,1)} %refs_4_.1, bf16[2,8,64]{2,1,0:T(8,128)(2,1)} %refs_5_.1, bf16[2,64,64]{2,1,0:T(8,128)(2,1)} %refs_6_.1, ...), custom_call_target="tpu_custom_call" | custom-call | tf_op jit(solution)/shard_map/pallas_call | solution.py:663
  42.6 0.6 %slice_bitcast_fusion.1 = f32[8,4,4]{0,2,1:T(4,128)} fusion(f32[4,4,4,8]{3,2,1,0:T(4,128)S(1)} %shard_map.158), kind=kLoop, calls=%fused_computation.1 | loop fusion | bytes 1024 | tf_op jit(solution)/shard_map/transpose | solution.py:712
  43.2 0.6 %slice_bitcast_fusion = f32[3,8,4,4]{1,3,2,0:T(4,128)} fusion(f32[4,4,4,8]{3,2,1,0:T(4,128)S(1)} %shard_map.158), kind=kLoop, calls=%fused_computation | loop fusion | bytes 3072 | tf_op jit(solution)/shard_map/transpose | solution.py:712
